TPU v7x, 128 devices: a whole 4x4x4 slice. The times are simulated.
128 devices in a mesh: tile: 16 (over x, z_lo, core), member: 8 (over z_hi, y).
Axes of the slice: x: 4, y: 4, z: 4 (z_hi: 2, z_lo: 2; z = z_hi * 2 + z_lo), core: 2. Of those that a mesh axis runs over, the one named last changes fastest.
Arguments:
- residual_in: float32 [64, 256, 1024], P(None, 'tile', 'member'), may hold values from -6 to 6
- members: bfloat16 [16, 64, 256, 1024], P('member', None, 'tile'), may hold values from -6 to 6
- wind_x: float32 [64], replicated, may hold values from 0.05 to 0.25
- wind_y: float32 [64], replicated, may hold values from 0.05 to 0.25
Outputs:
- analysis: float32 [64, 256, 1024], P(None, 'tile', 'member')
- residual: float32 [64, 256, 1024], P(None, 'tile', 'member')
All inputs are finite; a program needn't handle non-finite values.
Results may differ from a plain program's by a relative error of at most 0.006.
Values may be sent and summed in bfloat16 or wider, within the bound.
A program may use at most 64 MiB of HBM per device.

v0:
```python
import jax
import jax.numpy as jnp
from jax import lax
from jax.sharding import PartitionSpec as P

ITERS = 2
MODEL_STEPS = 4


diffusion = 0.1
relax = 0.5


def padded_2(block, sides, width):
    for axis, dim in sides:
        count = lax.axis_size(axis)
        forward = [(i, i + 1) for i in range(count - 1)]
        backward = [(target, source) for source, target in forward]
        low = lax.ppermute(
            lax.slice_in_dim(block, block.shape[dim] - width, None, axis=dim), axis, forward
        )
        high = lax.ppermute(lax.slice_in_dim(block, 0, width, axis=dim), axis, backward)
        block = jnp.concatenate([low, block, high], axis=dim)
    return block


def taper_weights():
    raw = [1.0 - (k / 17.0) ** 2 for k in range(-16, 17)]
    total = sum(raw)
    return [value / total for value in raw]


def advance(padded, wind_x, wind_y):
    center = padded[:, 1:-1, 1:-1]
    ahead_x = padded[:, 2:, 1:-1]
    behind_x = padded[:, :-2, 1:-1]
    ahead_y = padded[:, 1:-1, 2:]
    behind_y = padded[:, 1:-1, :-2]
    result = center + diffusion * (ahead_x + behind_x + ahead_y + behind_y - 4.0 * center)
    result = result - wind_x[:, None, None] * (center - ahead_x)
    return result - wind_y[:, None, None] * (center - ahead_y)


def smooth_axis(padded, count, axis):
    weights = taper_weights()
    total = weights[0] * lax.slice_in_dim(padded, 0, count, axis=axis)
    for offset in range(1, len(weights)):
        total = total + weights[offset] * lax.slice_in_dim(
            padded, offset, offset + count, axis=axis
        )
    return total


def adjoint_model(field, wind_x, wind_y):
    for sweep in range(MODEL_STEPS):
        padded = padded_2(field, (("tile", 1), ("member", 2)), 1)
        field = advance(padded, wind_x, wind_y)
    return field


def per_device(residual_in, members, wind_x, wind_y):
    residual = residual_in
    analysis = jnp.zeros_like(residual_in)
    block_rows = residual_in.shape[1]
    block_cols = residual_in.shape[2]
    total_cols = members.shape[3]
    members_f = members.astype(jnp.float32)
    for iteration in range(ITERS):
        grad = adjoint_model(residual, wind_x, wind_y).astype(jnp.bfloat16)
        gathered = lax.all_gather(grad, "member", axis=2, tiled=True).astype(jnp.float32)
        project = jnp.sum(members_f * gathered[None], axis=1)
        padded_rows = padded_2(project, (("tile", 1),), 16)
        smoothed = smooth_axis(padded_rows, block_rows, 1)
        localized = smooth_axis(jnp.pad(smoothed, ((0, 0), (0, 0), (16, 16))), total_cols, 2)
        partial_sum = jnp.sum(members_f * localized[:, None], axis=0)
        summed = lax.psum(partial_sum, "member")
        offset = lax.axis_index("member") * block_cols
        increment = lax.dynamic_slice_in_dim(summed, offset, block_cols, 2)
        analysis = analysis + increment
        residual = residual - relax * increment
    return (analysis, residual)


def solution(mesh):
    return jax.shard_map(
        per_device,
        mesh=mesh,
        in_specs=(P(None, "tile", "member"), P("member", None, "tile", None), P(), P()),
        out_specs=(P(None, "tile", "member"), P(None, "tile", "member")),
        check_vma=False,
    )
```

profile of v0, /device:TPU:29, one launch (start us, length us, event | category | flops | bytes accessed | tf_op | source)
XLA Modules:
  0.0 557.2 jit_solution(18177593108825092521)
XLA Ops:
  7.2 1.1 fusion.401
  8.4 4.1 collective-permute-start.1
  12.5 1.9 collective-permute-start
  14.4 3.3 collective-permute-done
  17.7 1.2 pad_maximum_fusion
  19.5 2.4 collective-permute-start.2
  22.1 6.5 %collective-permute-start.3 = (f32[64,18,1]{0,1,2:T(8,128)S(1)}, f32[64,18,1]{0,1,2:T(8,128)S(1)}, u32[]{:S(2)}, u32[]{:S(2)}) collective-permute-start(f32[64,18,1]{0,1,2:T(8,128)S(1)} %copy.140), channel_id=1, source_target_pairs={{0,1},{1,2},{2,3},{3,4},{4,5},{5,6},{6,7},{8,9},{9,10},{10,11},{11... | collective-permute-start | bytes 13832 | tf_op jit(solution)/shard_map/ppermute | solution.py:19
  30.7 3.0 collective-permute-start.5
  33.8 1.9 collective-permute-start.4
  35.7 3.3 collective-permute-done.4
  39.7 1.9 collective-permute-start.6
  42.0 8.3 %collective-permute-start.7 = (f32[64,18,1]{0,1,2:T(8,128)S(1)}, f32[64,18,1]{0,1,2:T(8,128)S(1)}, u32[]{:S(2)}, u32[]{:S(2)}) collective-permute-start(f32[64,18,1]{0,1,2:T(8,128)S(1)} %copy.144), channel_id=1, source_target_pairs={{0,1},{1,2},{2,3},{3,4},{4,5},{5,6},{6,7},{8,9},{9,10},{10,11},{11... | collective-permute-start | bytes 13832 | tf_op jit(solution)/shard_map/ppermute | solution.py:19
  52.3 2.2 collective-permute-start.9
  54.4 2.2 collective-permute-start.8
  56.6 3.0 collective-permute-done.8
  60.4 1.9 collective-permute-start.10
  62.6 8.1 %collective-permute-start.11 = (f32[64,18,1]{0,1,2:T(8,128)S(1)}, f32[64,18,1]{0,1,2:T(8,128)S(1)}, u32[]{:S(2)}, u32[]{:S(2)}) collective-permute-start(f32[64,18,1]{0,1,2:T(8,128)S(1)} %copy.148), channel_id=1, source_target_pairs={{0,1},{1,2},{2,3},{3,4},{4,5},{5,6},{6,7},{8,9},{9,10},{10,11},{11... | collective-permute-start | bytes 13832 | tf_op jit(solution)/shard_map/ppermute | solution.py:19
  72.8 2.2 collective-permute-start.13
  75.0 3.3 collective-permute-start.12
  78.3 2.3 collective-permute-done.12
  81.2 1.9 collective-permute-start.14
  83.5 7.8 %collective-permute-start.15 = (f32[64,18,1]{0,1,2:T(8,128)S(1)}, f32[64,18,1]{0,1,2:T(8,128)S(1)}, u32[]{:S(2)}, u32[]{:S(2)}) collective-permute-start(f32[64,18,1]{0,1,2:T(8,128)S(1)} %copy.152), channel_id=1, source_target_pairs={{0,1},{1,2},{2,3},{3,4},{4,5},{5,6},{6,7},{8,9},{9,10},{10,11},{11... | collective-permute-start | bytes 13832 | tf_op jit(solution)/shard_map/ppermute | solution.py:19
  92.5 1.5 fusion.51
  94.1 58.7 %all-gather.3.cloned.1.call-done = bf16[64,16,1024]{2,1,0:T(8,128)(2,1)} async-done(((bf16[64,16,128]{2,1,0:T(8,128)(2,1)}), bf16[64,16,1024]{2,1,0:T(8,128)(2,1)}) %all-gather.3.cloned.1.call-update) | async-done | bytes 2097168 | tf_op jit(solution)/shard_map/all_gather | solution.py:70
  152.7 2.2 convert_element_type.20
  155.6 1.1 fusion
  156.7 4.2 collective-permute-start.17
  160.9 2.4 collective-permute-start.16
  163.8 1.2 collective-permute-done.16
  165.5 1.1 multiply_add_fusion.1
  166.7 3.2 fusion.1
  169.9 108.3 %all-reduce.5.cloned.1.call-done = f32[64,16,1024]{2,1,0:T(8,128)} async-done(((f32[64,16,1024]{2,1,0:T(8,128)}), f32[64,16,1024]{2,1,0:T(8,128)}) %all-reduce.5.cloned.1.call-update) | async-done | bytes 4194320 | tf_op jit(solution)/shard_map/psum | solution.py:76
  278.3 1.1 multiply_subtract_fusion.1
  279.5 3.8 collective-permute-start.19
  283.3 1.9 collective-permute-start.18
  285.3 3.3 collective-permute-done.18
  289.3 1.9 collective-permute-start.20
  291.5 7.0 %collective-permute-start.21 = (f32[64,18,1]{0,1,2:T(8,128)S(1)}, f32[64,18,1]{0,1,2:T(8,128)S(1)}, u32[]{:S(2)}, u32[]{:S(2)}) collective-permute-start(f32[64,18,1]{0,1,2:T(8,128)S(1)} %copy.156), channel_id=1, source_target_pairs={{0,1},{1,2},{2,3},{3,4},{4,5},{5,6},{6,7},{8,9},{9,10},{10,11},{11... | collective-permute-start | bytes 13832 | tf_op jit(solution)/shard_map/ppermute | solution.py:19
  300.5 3.0 collective-permute-start.23
  303.6 1.9 collective-permute-start.22
  305.5 3.3 collective-permute-done.22
  309.5 1.9 collective-permute-start.24
  311.7 8.1 %collective-permute-start.25 = (f32[64,18,1]{0,1,2:T(8,128)S(1)}, f32[64,18,1]{0,1,2:T(8,128)S(1)}, u32[]{:S(2)}, u32[]{:S(2)}) collective-permute-start(f32[64,18,1]{0,1,2:T(8,128)S(1)} %copy.160), channel_id=1, source_target_pairs={{0,1},{1,2},{2,3},{3,4},{4,5},{5,6},{6,7},{8,9},{9,10},{10,11},{11... | collective-permute-start | bytes 13832 | tf_op jit(solution)/shard_map/ppermute | solution.py:19
  321.9 2.2 collective-permute-start.27
  324.1 2.8 collective-permute-start.26
  326.9 2.5 collective-permute-done.26
  330.1 1.9 collective-permute-start.28
  332.3 8.0 %collective-permute-start.29 = (f32[64,18,1]{0,1,2:T(8,128)S(1)}, f32[64,18,1]{0,1,2:T(8,128)S(1)}, u32[]{:S(2)}, u32[]{:S(2)}) collective-permute-start(f32[64,18,1]{0,1,2:T(8,128)S(1)} %copy.164), channel_id=1, source_target_pairs={{0,1},{1,2},{2,3},{3,4},{4,5},{5,6},{6,7},{8,9},{9,10},{10,11},{11... | collective-permute-start | bytes 13832 | tf_op jit(solution)/shard_map/ppermute | solution.py:19
  342.4 2.5 collective-permute-start.31
  344.9 3.4 collective-permute-start.30
  348.3 2.5 collective-permute-done.30
  351.5 1.9 collective-permute-start.32
  353.8 8.1 %collective-permute-start.33 = (f32[64,18,1]{0,1,2:T(8,128)S(1)}, f32[64,18,1]{0,1,2:T(8,128)S(1)}, u32[]{:S(2)}, u32[]{:S(2)}) collective-permute-start(f32[64,18,1]{0,1,2:T(8,128)S(1)} %copy.168), channel_id=1, source_target_pairs={{0,1},{1,2},{2,3},{3,4},{4,5},{5,6},{6,7},{8,9},{9,10},{10,11},{11... | collective-permute-start | bytes 13832 | tf_op jit(solution)/shard_map/ppermute | solution.py:19
  362.8 1.5 fusion.10
  364.3 58.5 %all-gather.5.cloned.1.call-done = bf16[64,16,1024]{2,1,0:T(8,128)(2,1)} async-done(((bf16[64,16,128]{2,1,0:T(8,128)(2,1)}), bf16[64,16,1024]{2,1,0:T(8,128)(2,1)}) %all-gather.5.cloned.1.call-update) | async-done | bytes 2097168 | tf_op jit(solution)/shard_map/all_gather | solution.py:70
  422.8 2.2 convert_element_type.22
  425.6 1.1 fusion.2
  426.8 4.2 collective-permute-start.35
  430.9 2.2 collective-permute-start.34
  433.8 1.2 collective-permute-done.34
  435.6 1.1 multiply_add_fusion
  436.7 3.2 fusion.3
  440.0 108.4 %all-reduce.7.cloned.1.call-done = f32[64,16,1024]{2,1,0:T(8,128)} async-done(((f32[64,16,1024]{2,1,0:T(8,128)}), f32[64,16,1024]{2,1,0:T(8,128)}) %all-reduce.7.cloned.1.call-update) | async-done | bytes 4194320 | tf_op jit(solution)/shard_map/psum | solution.py:76
  548.4 2.3 multiply_subtract_fusion
  (106 shorter events, 25.7 us)
Async XLA Ops:
  7.2 22.7 %copy-start.2 = (f32[64,16,128]{2,1,0:T(8,128)S(1)}, f32[64,16,128]{2,1,0:T(8,128)}, u32[]{:S(2)}) copy-start(f32[64,16,128]{2,1,0:T(8,128)} %param.4) | copy-start | bytes 1572868
  7.2 22.7 %copy-start.3 = (f32[64]{0:T(128)S(1)}, f32[64]{0:T(128)}, u32[]{:S(2)}) copy-start(f32[64]{0:T(128)} %param.7) | copy-start | bytes 772
  7.2 22.7 %copy-start.4 = (f32[64]{0:T(128)S(1)}, f32[64]{0:T(128)}, u32[]{:S(2)}) copy-start(f32[64]{0:T(128)} %param.6) | copy-start | bytes 772
  7.2 145.5 %all-gather.3.cloned.1.call-start = ((), (), s32[]{:S(2)}) async-start(), calls=%async_computation | async-start | bytes 2359296 | tf_op jit(solution)/shard_map/all_gather | solution.py:70
  8.4 6.0 %collective-permute-start.1 = (f32[64,1,128]{2,1,0:T(1,128)S(1)}, f32[64,1,128]{2,1,0:T(1,128)S(1)}, u32[]{:S(2)}, u32[]{:S(2)}) collective-permute-start(f32[64,1,128]{2,1,0:T(1,128)S(1)} %get-tuple-element.36), channel_id=1, source_target_pairs={{0,8},{8,16},{16,24},{24,32},{32,40},{40,48},{48,56},{56,64},{64,7... | collective-permute-start | bytes 98312 | tf_op jit(solution)/shard_map/ppermute | solution.py:19
  12.5 5.2 collective-permute-start
  19.5 9.2 %collective-permute-start.2 = (f32[64,18,1]{0,1,2:T(8,128)S(1)}, f32[64,18,1]{0,1,2:T(8,128)S(1)}, u32[]{:S(2)}, u32[]{:S(2)}) collective-permute-start(f32[64,18,1]{0,1,2:T(8,128)S(1)} %copy.138), channel_id=1, source_target_pairs={{1,0},{2,1},{3,2},{4,3},{5,4},{6,5},{7,6},{9,8},{10,9},{11,10},{12... | collective-permute-start | bytes 13832 | tf_op jit(solution)/shard_map/ppermute | solution.py:22
  22.1 7.3 %collective-permute-start.3 = (f32[64,18,1]{0,1,2:T(8,128)S(1)}, f32[64,18,1]{0,1,2:T(8,128)S(1)}, u32[]{:S(2)}, u32[]{:S(2)}) collective-permute-start(f32[64,18,1]{0,1,2:T(8,128)S(1)} %copy.140), channel_id=1, source_target_pairs={{0,1},{1,2},{2,3},{3,4},{4,5},{5,6},{6,7},{8,9},{9,10},{10,11},{11... | collective-permute-start | bytes 13832 | tf_op jit(solution)/shard_map/ppermute | solution.py:19
  30.7 5.0 collective-permute-start.5
  33.8 5.2 collective-permute-start.4
  39.7 10.5 %collective-permute-start.6 = (f32[64,18,1]{0,1,2:T(8,128)S(1)}, f32[64,18,1]{0,1,2:T(8,128)S(1)}, u32[]{:S(2)}, u32[]{:S(2)}) collective-permute-start(f32[64,18,1]{0,1,2:T(8,128)S(1)} %copy.142), channel_id=1, source_target_pairs={{1,0},{2,1},{3,2},{4,3},{5,4},{6,5},{7,6},{9,8},{10,9},{11,10},{12... | collective-permute-start | bytes 13832 | tf_op jit(solution)/shard_map/ppermute | solution.py:22
  42.0 9.1 %collective-permute-start.7 = (f32[64,18,1]{0,1,2:T(8,128)S(1)}, f32[64,18,1]{0,1,2:T(8,128)S(1)}, u32[]{:S(2)}, u32[]{:S(2)}) collective-permute-start(f32[64,18,1]{0,1,2:T(8,128)S(1)} %copy.144), channel_id=1, source_target_pairs={{0,1},{1,2},{2,3},{3,4},{4,5},{5,6},{6,7},{8,9},{9,10},{10,11},{11... | collective-permute-start | bytes 13832 | tf_op jit(solution)/shard_map/ppermute | solution.py:19
  52.3 4.3 collective-permute-start.9
  54.4 5.2 collective-permute-start.8
  60.4 10.4 %collective-permute-start.10 = (f32[64,18,1]{0,1,2:T(8,128)S(1)}, f32[64,18,1]{0,1,2:T(8,128)S(1)}, u32[]{:S(2)}, u32[]{:S(2)}) collective-permute-start(f32[64,18,1]{0,1,2:T(8,128)S(1)} %copy.146), channel_id=1, source_target_pairs={{1,0},{2,1},{3,2},{4,3},{5,4},{6,5},{7,6},{9,8},{10,9},{11,10},{12... | collective-permute-start | bytes 13832 | tf_op jit(solution)/shard_map/ppermute | solution.py:22
  62.6 9.0 %collective-permute-start.11 = (f32[64,18,1]{0,1,2:T(8,128)S(1)}, f32[64,18,1]{0,1,2:T(8,128)S(1)}, u32[]{:S(2)}, u32[]{:S(2)}) collective-permute-start(f32[64,18,1]{0,1,2:T(8,128)S(1)} %copy.148), channel_id=1, source_target_pairs={{0,1},{1,2},{2,3},{3,4},{4,5},{5,6},{6,7},{8,9},{9,10},{10,11},{11... | collective-permute-start | bytes 13832 | tf_op jit(solution)/shard_map/ppermute | solution.py:19
  72.8 5.5 collective-permute-start.13
  75.0 5.6 %collective-permute-start.12 = (f32[64,1,128]{2,1,0:T(1,128)S(1)}, f32[64,1,128]{2,1,0:T(1,128)S(1)}, u32[]{:S(2)}, u32[]{:S(2)}) collective-permute-start(f32[64,1,128]{2,1,0:T(1,128)S(1)} %get-tuple-element.31), channel_id=1, source_target_pairs={{8,0},{16,8},{24,16},{32,24},{40,32},{48,40},{56,48},{64,56},{72,6... | collective-permute-start | bytes 98312 | tf_op jit(solution)/shard_map/ppermute | solution.py:22
  81.2 10.1 %collective-permute-start.14 = (f32[64,18,1]{0,1,2:T(8,128)S(1)}, f32[64,18,1]{0,1,2:T(8,128)S(1)}, u32[]{:S(2)}, u32[]{:S(2)}) collective-permute-start(f32[64,18,1]{0,1,2:T(8,128)S(1)} %copy.150), channel_id=1, source_target_pairs={{1,0},{2,1},{3,2},{4,3},{5,4},{6,5},{7,6},{9,8},{10,9},{11,10},{12... | collective-permute-start | bytes 13832 | tf_op jit(solution)/shard_map/ppermute | solution.py:22
  83.5 8.7 %collective-permute-start.15 = (f32[64,18,1]{0,1,2:T(8,128)S(1)}, f32[64,18,1]{0,1,2:T(8,128)S(1)}, u32[]{:S(2)}, u32[]{:S(2)}) collective-permute-start(f32[64,18,1]{0,1,2:T(8,128)S(1)} %copy.152), channel_id=1, source_target_pairs={{0,1},{1,2},{2,3},{3,4},{4,5},{5,6},{6,7},{8,9},{9,10},{10,11},{11... | collective-permute-start | bytes 13832 | tf_op jit(solution)/shard_map/ppermute | solution.py:19
  94.0 184.3 %all-reduce.5.cloned.1.call-start = ((), (), s32[]{:S(2)}) async-start(), calls=%async_computation.1 | async-start | bytes 8388608 | tf_op jit(solution)/shard_map/psum | solution.py:76
  152.7 2.8 copy-start
  156.7 7.1 %collective-permute-start.17 = (f32[2,16,1024]{2,1,0:T(8,128)S(1)}, f32[2,16,1024]{2,1,0:T(8,128)S(1)}, u32[]{:S(2)}, u32[]{:S(2)}) collective-permute-start(f32[2,16,1024]{2,1,0:T(8,128)S(1)} %fusion), channel_id=1, source_target_pairs={{8,0},{16,8},{24,16},{32,24},{40,32},{48,40},{56,48},{64,56},{72,6... | collective-permute-start | bytes 393224 | tf_op jit(solution)/shard_map/ppermute | solution.py:22
  160.9 4.1 collective-permute-start.16
  169.9 252.9 %all-gather.5.cloned.1.call-start = ((), (), s32[]{:S(2)}) async-start(), calls=%async_computation.2 | async-start | bytes 2359296 | tf_op jit(solution)/shard_map/all_gather | solution.py:70
  279.5 5.8 %collective-permute-start.19 = (f32[64,1,128]{2,1,0:T(1,128)S(1)}, f32[64,1,128]{2,1,0:T(1,128)S(1)}, u32[]{:S(2)}, u32[]{:S(2)}) collective-permute-start(f32[64,1,128]{2,1,0:T(1,128)S(1)} %get-tuple-element.28), channel_id=1, source_target_pairs={{0,8},{8,16},{16,24},{24,32},{32,40},{40,48},{48,56},{56,64},{64,7... | collective-permute-start | bytes 98312 | tf_op jit(solution)/shard_map/ppermute | solution.py:19
  283.3 5.2 collective-permute-start.18
  289.3 9.2 %collective-permute-start.20 = (f32[64,18,1]{0,1,2:T(8,128)S(1)}, f32[64,18,1]{0,1,2:T(8,128)S(1)}, u32[]{:S(2)}, u32[]{:S(2)}) collective-permute-start(f32[64,18,1]{0,1,2:T(8,128)S(1)} %copy.154), channel_id=1, source_target_pairs={{1,0},{2,1},{3,2},{4,3},{5,4},{6,5},{7,6},{9,8},{10,9},{11,10},{12... | collective-permute-start | bytes 13832 | tf_op jit(solution)/shard_map/ppermute | solution.py:22
  291.5 7.8 %collective-permute-start.21 = (f32[64,18,1]{0,1,2:T(8,128)S(1)}, f32[64,18,1]{0,1,2:T(8,128)S(1)}, u32[]{:S(2)}, u32[]{:S(2)}) collective-permute-start(f32[64,18,1]{0,1,2:T(8,128)S(1)} %copy.156), channel_id=1, source_target_pairs={{0,1},{1,2},{2,3},{3,4},{4,5},{5,6},{6,7},{8,9},{9,10},{10,11},{11... | collective-permute-start | bytes 13832 | tf_op jit(solution)/shard_map/ppermute | solution.py:19
  300.5 5.0 collective-permute-start.23
  303.6 5.2 collective-permute-start.22
  309.5 10.4 %collective-permute-start.24 = (f32[64,18,1]{0,1,2:T(8,128)S(1)}, f32[64,18,1]{0,1,2:T(8,128)S(1)}, u32[]{:S(2)}, u32[]{:S(2)}) collective-permute-start(f32[64,18,1]{0,1,2:T(8,128)S(1)} %copy.158), channel_id=1, source_target_pairs={{1,0},{2,1},{3,2},{4,3},{5,4},{6,5},{7,6},{9,8},{10,9},{11,10},{12... | collective-permute-start | bytes 13832 | tf_op jit(solution)/shard_map/ppermute | solution.py:22
  311.7 9.0 %collective-permute-start.25 = (f32[64,18,1]{0,1,2:T(8,128)S(1)}, f32[64,18,1]{0,1,2:T(8,128)S(1)}, u32[]{:S(2)}, u32[]{:S(2)}) collective-permute-start(f32[64,18,1]{0,1,2:T(8,128)S(1)} %copy.160), channel_id=1, source_target_pairs={{0,1},{1,2},{2,3},{3,4},{4,5},{5,6},{6,7},{8,9},{9,10},{10,11},{11... | collective-permute-start | bytes 13832 | tf_op jit(solution)/shard_map/ppermute | solution.py:19
  321.9 5.0 collective-permute-start.27
  324.1 5.3 collective-permute-start.26
  330.1 10.3 %collective-permute-start.28 = (f32[64,18,1]{0,1,2:T(8,128)S(1)}, f32[64,18,1]{0,1,2:T(8,128)S(1)}, u32[]{:S(2)}, u32[]{:S(2)}) collective-permute-start(f32[64,18,1]{0,1,2:T(8,128)S(1)} %copy.162), channel_id=1, source_target_pairs={{1,0},{2,1},{3,2},{4,3},{5,4},{6,5},{7,6},{9,8},{10,9},{11,10},{12... | collective-permute-start | bytes 13832 | tf_op jit(solution)/shard_map/ppermute | solution.py:22
  332.3 8.9 %collective-permute-start.29 = (f32[64,18,1]{0,1,2:T(8,128)S(1)}, f32[64,18,1]{0,1,2:T(8,128)S(1)}, u32[]{:S(2)}, u32[]{:S(2)}) collective-permute-start(f32[64,18,1]{0,1,2:T(8,128)S(1)} %copy.164), channel_id=1, source_target_pairs={{0,1},{1,2},{2,3},{3,4},{4,5},{5,6},{6,7},{8,9},{9,10},{10,11},{11... | collective-permute-start | bytes 13832 | tf_op jit(solution)/shard_map/ppermute | solution.py:19
  342.4 5.9 %collective-permute-start.31 = (f32[64,1,128]{2,1,0:T(1,128)S(1)}, f32[64,1,128]{2,1,0:T(1,128)S(1)}, u32[]{:S(2)}, u32[]{:S(2)}) collective-permute-start(f32[64,1,128]{2,1,0:T(1,128)S(1)} %get-tuple-element.22), channel_id=1, source_target_pairs={{0,8},{8,16},{16,24},{24,32},{32,40},{40,48},{48,56},{56,64},{64,7... | collective-permute-start | bytes 98312 | tf_op jit(solution)/shard_map/ppermute | solution.py:19
  344.9 5.9 %collective-permute-start.30 = (f32[64,1,128]{2,1,0:T(1,128)S(1)}, f32[64,1,128]{2,1,0:T(1,128)S(1)}, u32[]{:S(2)}, u32[]{:S(2)}) collective-permute-start(f32[64,1,128]{2,1,0:T(1,128)S(1)} %get-tuple-element.23), channel_id=1, source_target_pairs={{8,0},{16,8},{24,16},{32,24},{40,32},{48,40},{56,48},{64,56},{72,6... | collective-permute-start | bytes 98312 | tf_op jit(solution)/shard_map/ppermute | solution.py:22
  351.5 10.3 %collective-permute-start.32 = (f32[64,18,1]{0,1,2:T(8,128)S(1)}, f32[64,18,1]{0,1,2:T(8,128)S(1)}, u32[]{:S(2)}, u32[]{:S(2)}) collective-permute-start(f32[64,18,1]{0,1,2:T(8,128)S(1)} %copy.166), channel_id=1, source_target_pairs={{1,0},{2,1},{3,2},{4,3},{5,4},{6,5},{7,6},{9,8},{10,9},{11,10},{12... | collective-permute-start | bytes 13832 | tf_op jit(solution)/shard_map/ppermute | solution.py:22
  353.8 8.7 %collective-permute-start.33 = (f32[64,18,1]{0,1,2:T(8,128)S(1)}, f32[64,18,1]{0,1,2:T(8,128)S(1)}, u32[]{:S(2)}, u32[]{:S(2)}) collective-permute-start(f32[64,18,1]{0,1,2:T(8,128)S(1)} %copy.168), channel_id=1, source_target_pairs={{0,1},{1,2},{2,3},{3,4},{4,5},{5,6},{6,7},{8,9},{9,10},{10,11},{11... | collective-permute-start | bytes 13832 | tf_op jit(solution)/shard_map/ppermute | solution.py:19
  364.3 184.1 %all-reduce.7.cloned.1.call-start = ((), (), s32[]{:S(2)}) async-start(), calls=%async_computation.3 | async-start | bytes 8388608 | tf_op jit(solution)/shard_map/psum | solution.py:76
  422.8 2.8 copy-start.1
  426.8 7.1 %collective-permute-start.35 = (f32[2,16,1024]{2,1,0:T(8,128)S(1)}, f32[2,16,1024]{2,1,0:T(8,128)S(1)}, u32[]{:S(2)}, u32[]{:S(2)}) collective-permute-start(f32[2,16,1024]{2,1,0:T(8,128)S(1)} %fusion.2), channel_id=1, source_target_pairs={{8,0},{16,8},{24,16},{32,24},{40,32},{48,40},{56,48},{64,56},{72,6... | collective-permute-start | bytes 393224 | tf_op jit(solution)/shard_map/ppermute | solution.py:22
  430.9 4.1 collective-permute-start.34
Sparse Core Ops, SparseCore 0:
  94.1 58.5 all-gather.2
  170.0 108.2 all-reduce.4
  364.4 58.3 all-gather.4
  440.1 108.2 all-reduce.6
where the time goes:
time: 562 us; the launch traced here: 557 us
  waiting for transfers between devices  364 us (65%)
  starting transfers between devices  133 us (24%)
  other arithmetic  29.6 us (5%)
  local copies, waits for them, and re-layouts  15.3 us (3%)
  between operations  14.5 us (3%)
    psum x2, waiting for transfers between devices, per_device(): summed = lax.psum(partial_sum, 'member')  217 us
    all_gather x2, waiting for transfers between devices, per_device(): lax.all_gather(grad, 'member', axis=2, tiled=True).astype(jnp.float32)  117 us
    ppermute x18, starting transfers between devices, padded_2(): lax.ppermute(lax.slice_in_dim(block, block.shape[dim] - width, None, axis...  89.6 us
    ppermute x18, starting transfers between devices, padded_2(): lax.ppermute(lax.slice_in_dim(block, 0, width, axis=dim), axis, backward)  43.5 us
    ppermute x18, waiting for transfers between devices, padded_2(): lax.ppermute(lax.slice_in_dim(block, 0, width, axis=dim), axis, backward)  24.8 us
  transfers between devices with their start and end apart: 40, of which 24 were waited for; matrix products, arithmetic and copies ran while one was open for 1% of the time, Pallas kernels for 0%

commit v1 on v0

v1 whole, which is shorter than its diff:
```python
import functools

import jax
import jax.numpy as jnp
from jax import lax
from jax.experimental import pallas as pl
from jax.experimental.pallas import tpu as pltpu
from jax.sharding import PartitionSpec as P

MESH = pl.DeviceIdType.MESH
F32 = jnp.float32
BF16 = jnp.bfloat16

LEV = 64
ROWS = 16
COLS = 128
GROUPS = LEV // 8
STEPS = 4
HALO = STEPS
XROWS = ROWS + 2 * HALO
REACH = 16
CHUNKS = 4
CLEV = LEV // CHUNKS

diffusion = 0.1
relax = 0.5

FLOWS = ((2, 1), (1, 1), (3, 1), (0, 1), (2, 0), (1, 0), (3, 0))
SIDES = ((1, 0), (-1, 0), (0, 1), (0, -1), (1, 1), (-1, 1), (1, -1), (-1, -1))


def taper_weights():
    raw = [1.0 - (k / 17.0) ** 2 for k in range(-16, 17)]
    total = sum(raw)
    return [value / total for value in raw]


def kernel(
    tiles, blocks,
    res_hbm, mem_hbm, wx_ref, wy_ref,
    ana_ref,
    res, mt, a0, a1, w1, w2, c0, ax, ay, own, strip, mr, ml, ql, qr, gt, g,
    proj, sx, pk_r, pk_l, cl, cr, hx, band, z,
    own_sem, res_sem, m_send, m_recv, h_send, h_recv, p_send, p_recv, c_send, c_recv,
):
    t = lax.axis_index("tile")
    m = lax.axis_index("member")
    zh, y = m // 4, m % 4
    w = taper_weights()

    def there(dt, dm):
        ok = None
        for cond in ([t < tiles - 1] if dt > 0 else [t > 0] if dt < 0 else []) + (
            [m < blocks - 1] if dm > 0 else [m > 0] if dm < 0 else []
        ):
            ok = cond if ok is None else jnp.logical_and(ok, cond)
        return ok

    def peer(dt, dm):
        return ((t + dt + tiles) % tiles, (m + dm + blocks) % blocks)

    def mate(dy, dz):
        return ((zh + dz) % 2) * 4 + (y + dy + 4) % 4

    res_copy = pltpu.make_async_copy(res_hbm, res, res_sem)
    res_copy.start()
    own_copy = pltpu.make_async_copy(
        mem_hbm.at[:, :, :, pl.ds(pl.multiple_of(m * COLS, COLS), COLS)], mt.at[m], own_sem
    )
    own_copy.start()

    barrier = pltpu.get_barrier_semaphore()
    count = jnp.int32(len(FLOWS))
    for dy, dz in FLOWS:
        pl.semaphore_signal(barrier, inc=1, device_id=(t, mate(dy, dz)), device_id_type=MESH)
    for dt, dm in SIDES:
        if dt == 0:
            continue
        ok = there(dt, dm)
        count = count + ok.astype(jnp.int32)

        @pl.when(ok)
        def _():
            pl.semaphore_signal(barrier, inc=1, device_id=peer(dt, dm), device_id_type=MESH)

    pl.semaphore_wait(barrier, count)

    def member_copy(i, c):
        dy, dz = FLOWS[i]
        target = mate(dy, dz)
        return pltpu.make_async_remote_copy(
            src_ref=mem_hbm.at[
                :, pl.ds(c * CLEV, CLEV), :, pl.ds(pl.multiple_of(target * COLS, COLS), COLS)
            ],
            dst_ref=mt.at[m, :, pl.ds(c * CLEV, CLEV)],
            send_sem=m_send.at[i, c],
            recv_sem=m_recv.at[i, c],
            device_id=(t, target),
            device_id_type=MESH,
        )

    for i in range(len(FLOWS)):
        member_copy(i, 0).start()

    @pl.when(t == 0)
    def _():
        for a in (a0, a1):
            a[pl.ds(0, HALO * LEV), :] = jnp.zeros((HALO * LEV, COLS), F32)
        ql[:, 0] = jnp.zeros((2, 8, COLS), F32)
        qr[:, 0] = jnp.zeros((2, 8, COLS), F32)
        proj[:, :, 0:REACH, :] = jnp.zeros((2, 16, REACH, COLS), F32)

    @pl.when(t == tiles - 1)
    def _():
        for a in (a0, a1):
            a[pl.ds((HALO + ROWS) * LEV, HALO * LEV), :] = jnp.zeros((HALO * LEV, COLS), F32)
        ql[:, 5] = jnp.zeros((2, 8, COLS), F32)
        qr[:, 5] = jnp.zeros((2, 8, COLS), F32)
        proj[:, :, REACH + ROWS :, :] = jnp.zeros((2, 16, REACH, COLS), F32)

    @pl.when(m == 0)
    def _():
        ql[...] = jnp.zeros(ql.shape, F32)
        cl[...] = jnp.zeros(cl.shape, F32)

    @pl.when(m == blocks - 1)
    def _():
        qr[...] = jnp.zeros(qr.shape, F32)
        cr[...] = jnp.zeros(cr.shape, F32)

    lane = lax.broadcasted_iota(jnp.int32, (8, COLS), 1)
    q = lane % 16
    group = lane // 16

    def quad_copy(it, d):
        a = (a0, a1)[it]
        dt, dm = SIDES[d]
        if dm == 0:
            rows = HALO * LEV
            src = a.at[pl.ds(ROWS * LEV if dt > 0 else HALO * LEV, rows)]
            dst = a.at[pl.ds(0 if dt > 0 else (HALO + ROWS) * LEV, rows)]
        else:
            src, dst = (mr.at[it], ql.at[it]) if dm > 0 else (ml.at[it], qr.at[it])
            if dt == 0:
                src, dst = src, dst.at[pl.ds(1, 4)]
            elif dt > 0:
                src, dst = src.at[pl.ds(3, 1)], dst.at[pl.ds(0, 1)]
            else:
                src, dst = src.at[pl.ds(0, 1)], dst.at[pl.ds(5, 1)]
        return pltpu.make_async_remote_copy(
            src_ref=src, dst_ref=dst, send_sem=h_send.at[it, d], recv_sem=h_recv.at[it, d],
            device_id=peer(dt, dm), device_id_type=MESH,
        )

    def guarded(ok, action):
        if ok is None:
            action()
        else:
            pl.when(ok)(action)

    def edges(a, r):
        total = jnp.zeros((8, COLS), F32)
        for k in range(GROUPS):
            v = a[pl.ds(pl.multiple_of(r * LEV + 8 * k, 8), 8), :]
            low = pltpu.roll(v, (16 * k + 4) % COLS, 1)
            high = pltpu.roll(v, (16 * k + 12) % COLS, 1)
            part = jnp.where(q < 8, low, high)
            total = jnp.where(group == k, part, total)
        return total

    def send_halos(it):
        a = (a0, a1)[it]
        for d in (0, 1):
            guarded(there(*SIDES[d]), quad_copy(it, d).start)

        def pack(r, carry):
            own[HALO + r] = edges(a, HALO + r)
            return carry

        lax.fori_loop(0, ROWS, pack, 0)
        for quad in range(4):
            right = jnp.zeros((8, COLS), F32)
            left = jnp.zeros((8, COLS), F32)
            for k in range(4):
                v = own[HALO + 4 * quad + k]
                here = q // 4 == k
                right = jnp.where(here, pltpu.roll(v, (4 * k - 8) % COLS, 1), right)
                left = jnp.where(here, pltpu.roll(v, (4 * k - 4) % COLS, 1), left)
            mr[it, quad] = right
            ml[it, quad] = left
        for d in range(2, 8):
            guarded(there(*SIDES[d]), quad_copy(it, d).start)

    res_copy.wait()

    def spread(l, carry):
        v = res[l]
        a0[pl.ds(HALO * LEV + l, 8, stride=LEV), :] = v[0:8]
        a0[pl.ds((HALO + 8) * LEV + l, 8, stride=LEV), :] = v[8:16]
        return carry

    lax.fori_loop(0, LEV, spread, 0, unroll=4)
    send_halos(0)
    for c in range(1, CHUNKS):
        for i in range(len(FLOWS)):
            member_copy(i, c).start()

    def coefficients(l, carry):
        wx, wy = wx_ref[l], wy_ref[l]
        c0[pl.ds(l, 1), :] = jnp.full((1, COLS), (1.0 - 4.0 * diffusion - wx - wy) / diffusion, F32)
        ax[pl.ds(l, 1), :] = jnp.full((1, COLS), (diffusion + wx) / diffusion, F32)
        ay[pl.ds(l, 1), :] = jnp.full((1, COLS), (diffusion + wy) / diffusion, F32)
        return carry

    lax.fori_loop(0, LEV, coefficients, 0)

    j = lax.broadcasted_iota(jnp.int32, (2 * COLS, COLS), 0)
    k = jnp.where(j < COLS + COLS // 2, j, j - 2 * COLS) - lax.broadcasted_iota(
        jnp.int32, (2 * COLS, COLS), 1
    )
    total_w = sum(1.0 - (i / 17.0) ** 2 for i in range(-16, 17))
    kf = k.astype(F32)
    full = jnp.where(jnp.abs(k) <= REACH, (1.0 - kf * kf * (1.0 / 289.0)) * (1.0 / total_w), 0.0)
    coarse = full.astype(BF16)
    band[0] = coarse
    band[1] = (full - coarse.astype(F32)).astype(BF16)

    def strip_coefficient(ref):
        total = jnp.zeros((8, COLS), F32)
        for k in range(GROUPS):
            total = jnp.where(group == k, ref[8 * k : 8 * k + 8, :], total)
        return total

    row_low = jnp.where(t > 0, 1.0, 0.0).astype(F32)
    row_high = jnp.where(t < tiles - 1, 1.0, 0.0).astype(F32)
    inside = jnp.logical_and(
        jnp.logical_or(q >= 4, m > 0), jnp.logical_or(q < 12, m < blocks - 1)
    )
    strip_mask = jnp.where(inside, 1.0, 0.0).astype(F32)

    def adjoint(it):
        a = (a0, a1)[it]
        for d in range(8):
            dt, dm = SIDES[d]
            guarded(there(-dt, -dm), quad_copy(it, d).wait_recv)

        def pack(r, carry):
            own[r] = edges(a, r)
            own[r + HALO + ROWS] = edges(a, r + HALO + ROWS)
            return carry

        lax.fori_loop(0, HALO, pack, 0)
        for r in range(XROWS):
            left = pltpu.roll(ql[it, r // 4], (-4 * (r % 4)) % COLS, 1)
            right = pltpu.roll(qr[it, r // 4], (12 - 4 * (r % 4)) % COLS, 1)
            strip[0, r] = jnp.where(q < 4, left, jnp.where(q >= 12, right, own[r]))
        sc0, sax, say = strip_coefficient(c0), strip_coefficient(ax), strip_coefficient(ay)
        for step in range(1, STEPS):
            for r in range(step, XROWS - step):
                v = strip[step - 1, r]
                out = (
                    sc0 * v
                    + (strip[step - 1, r - 1] + pltpu.roll(v, 1, 1))
                    + sax * strip[step - 1, r + 1]
                    + say * pltpu.roll(v, COLS - 1, 1)
                ) * strip_mask
                if r < HALO:
                    out = out * row_low
                elif r >= HALO + ROWS:
                    out = out * row_high
                strip[step, r] = out
        for step in range(1, STEPS + 1):
            src = (a, w1, w2, w1)[step - 1]
            dst = (w1, w2, w1, gt)[step - 1]

            def row(r, carry, scale=None):
                side = strip[step - 1, r]
                for k in range(GROUPS):
                    at = r * LEV + 8 * k
                    here = pl.ds(pl.multiple_of(at, 8), 8)
                    v = src[here, :]
                    up = src[pl.ds(pl.multiple_of(at - LEV, 8), 8), :]
                    down = src[pl.ds(pl.multiple_of(at + LEV, 8), 8), :]
                    left = jnp.where(
                        lane == 0, pltpu.roll(side, (-(16 * k + 3)) % COLS, 1), pltpu.roll(v, 1, 1)
                    )
                    right = jnp.where(
                        lane == COLS - 1,
                        pltpu.roll(side, (COLS - 1 - (16 * k + 12)) % COLS, 1),
                        pltpu.roll(v, COLS - 1, 1),
                    )
                    s = slice(8 * k, 8 * k + 8)
                    out = c0[s, :] * v + (up + left) + ax[s, :] * down + ay[s, :] * right
                    if scale is not None:
                        out = out * scale
                    if step == STEPS:
                        out = (out * diffusion**STEPS).astype(BF16).astype(F32)
                        dst[pl.ds(pl.multiple_of(at - HALO * LEV, 8), 8), :] = out
                    else:
                        dst[here, :] = out
                return carry

            if step < STEPS:
                lax.fori_loop(step, HALO, functools.partial(row, scale=row_low), 0)
            lax.fori_loop(HALO, HALO + ROWS, row, 0)
            if step < STEPS:
                lax.fori_loop(
                    HALO + ROWS, XROWS - step, functools.partial(row, scale=row_high), 0
                )

        def gather(l, carry):
            g[l, 0:8, :] = gt[pl.ds(l, 8, stride=LEV), :]
            g[l, 8:16, :] = gt[pl.ds(8 * LEV + l, 8, stride=LEV), :]
            return carry

        lax.fori_loop(0, LEV, gather, 0, unroll=4)

    own_rows = pl.ds(REACH, ROWS)

    def project(it, pair, first, count, fresh):
        if fresh:
            start = (jnp.zeros((ROWS, COLS), F32), jnp.zeros((ROWS, COLS), F32))
        else:
            start = (proj[it, 2 * pair, own_rows, :], proj[it, 2 * pair + 1, own_rows, :])

        def level(l, sums):
            v = g[l]
            return tuple(s + mt[pair, n, l].astype(F32) * v for n, s in enumerate(sums))

        sums = lax.fori_loop(first, first + count, level, start, unroll=4)
        for n in range(2):
            proj[it, 2 * pair + n, own_rows, :] = sums[n]

    def project_copy(it, pair, slot, d):
        return pltpu.make_async_remote_copy(
            src_ref=proj.at[it, pl.ds(2 * pair, 2), own_rows],
            dst_ref=proj.at[it, pl.ds(2 * pair, 2), pl.ds(0 if d == 0 else REACH + ROWS, REACH)],
            send_sem=p_send.at[it, slot, d], recv_sem=p_recv.at[it, slot, d],
            device_id=peer(*SIDES[d]), device_id_type=MESH,
        )

    pairs = [m] + [mate(-dy, dz) for dy, dz in FLOWS]

    def send_project(it, slot):
        for d in (0, 1):
            guarded(there(*SIDES[d]), project_copy(it, pairs[slot], slot, d).start)

    def smooth_rows(it, slot):
        pair = pairs[slot]
        for d in (0, 1):
            dt, dm = SIDES[d]
            guarded(there(-dt, -dm), project_copy(it, pair, slot, d).wait_recv)
        for n in range(2):
            for half in (0, 8):
                at = REACH + half
                total = w[REACH] * proj[it, 2 * pair + n, pl.ds(at, 8), :]
                for k in range(1, REACH + 1):
                    total = total + w[REACH + k] * (
                        proj[it, 2 * pair + n, pl.ds(at - k, 8), :]
                        + proj[it, 2 * pair + n, pl.ds(at + k, 8), :]
                    )
                sx[pl.ds(pl.multiple_of((2 * pair + n) * ROWS + half, 8), 8), :] = total

    def column_copy(it, d):
        src, dst = (pk_r.at[it], cl.at[it]) if d == 0 else (pk_l.at[it], cr.at[it])
        return pltpu.make_async_remote_copy(
            src_ref=src, dst_ref=dst, send_sem=c_send.at[it, d], recv_sem=c_recv.at[it, d],
            device_id=peer(0, 1 if d == 0 else -1), device_id_type=MESH,
        )

    def split(x):
        high = x.astype(BF16)
        return high, (x - high.astype(F32)).astype(BF16)

    def times(x, part):
        high, low = split(x)
        rows = slice(part * COLS, part * COLS + COLS)
        b_high, b_low = band[0, rows, :], band[1, rows, :]
        dot = functools.partial(jnp.dot, preferred_element_type=F32)
        return dot(high, b_high) + (dot(low, b_high) + dot(high, b_low))

    def smooth_columns(it):
        for part in range(2):
            for half in (0, 8):
                right = jnp.zeros((8, COLS), F32)
                left = jnp.zeros((8, COLS), F32)
                for n in range(8):
                    at = (8 * part + n) * ROWS + half
                    v = sx[at : at + 8, :]
                    right = jnp.where(group == n, pltpu.roll(v, (16 * n - 112) % COLS, 1), right)
                    left = jnp.where(group == n, pltpu.roll(v, 16 * n, 1), left)
                at = part * ROWS + half
                pk_r[it, at : at + 8, :] = right
                pk_l[it, at : at + 8, :] = left
        guarded(there(0, 1), column_copy(it, 0).start)
        guarded(there(0, -1), column_copy(it, 1).start)
        z[...] = times(sx[...], 0)
        guarded(there(0, -1), column_copy(it, 0).wait_recv)
        guarded(there(0, 1), column_copy(it, 1).wait_recv)
        for part in range(2):
            for half in (0, 8):
                at = part * ROWS + half
                from_left = cl[it, at : at + 8, :]
                from_right = cr[it, at : at + 8, :]
                for n in range(8):
                    to = (8 * part + n) * ROWS + half
                    hx[to : to + 8, :] = jnp.where(
                        lane < 16,
                        pltpu.roll(from_right, (-16 * n) % COLS, 1),
                        jnp.where(lane >= 112, pltpu.roll(from_left, (112 - 16 * n) % COLS, 1), 0.0),
                    )
        z[...] = z[...] + times(hx[...], 1)

    def increments(it):
        width = 2

        def levels(step, carry):
            sums = [jnp.zeros((ROWS, COLS), F32) for _ in range(width)]
            for pair in range(8):
                for n in range(2):
                    v = z[pl.ds((2 * pair + n) * ROWS, ROWS), :]
                    for i in range(width):
                        sums[i] = sums[i] + mt[pair, n, width * step + i].astype(F32) * v
            for i in range(width):
                l = width * step + i
                if it == 0:
                    ana_ref[l] = sums[i]
                    v = res[l] - relax * sums[i]
                    a1[pl.ds(HALO * LEV + l, 8, stride=LEV), :] = v[0:8]
                    a1[pl.ds((HALO + 8) * LEV + l, 8, stride=LEV), :] = v[8:16]
                else:
                    ana_ref[l] = ana_ref[l] + sums[i]
            return carry

        lax.fori_loop(0, LEV // width, levels, 0)

    adjoint(0)
    own_copy.wait()
    project(0, pairs[0], 0, LEV, True)
    send_project(0, 0)
    for c in range(CHUNKS):
        for i in range(len(FLOWS)):
            member_copy(i, c).wait_recv()
            project(0, pairs[1 + i], c * CLEV, CLEV, c == 0)
            if c == CHUNKS - 1:
                send_project(0, 1 + i)
    for slot in range(8):
        smooth_rows(0, slot)
    smooth_columns(0)
    increments(0)

    send_halos(1)
    adjoint(1)
    for slot in range(8):
        project(1, pairs[slot], 0, LEV, True)
        send_project(1, slot)
    for slot in range(8):
        smooth_rows(1, slot)
    smooth_columns(1)
    increments(1)

    for c in range(CHUNKS):
        for i in range(len(FLOWS)):
            member_copy(i, c).wait_send()
    for it in range(2):
        for d in range(8):
            guarded(there(*SIDES[d]), quad_copy(it, d).wait_send)
        for slot in range(8):
            for d in (0, 1):
                guarded(there(*SIDES[d]), project_copy(it, pairs[slot], slot, d).wait_send)
        guarded(there(0, 1), column_copy(it, 0).wait_send)
        guarded(there(0, -1), column_copy(it, 1).wait_send)


def per_device(tiles, blocks, residual_in, members, wind_x, wind_y):
    vmem = pltpu.VMEM
    dma = lambda *shape: pltpu.SemaphoreType.DMA(shape)
    anywhere = pl.BlockSpec(memory_space=pl.ANY)
    scalars = pl.BlockSpec(memory_space=pltpu.SMEM)
    extended = vmem((XROWS * LEV, COLS), F32)
    coefficient = vmem((LEV, COLS), F32)
    analysis = pl.pallas_call(
        functools.partial(kernel, tiles, blocks),
        out_shape=jax.ShapeDtypeStruct((LEV, ROWS, COLS), F32),
        in_specs=[anywhere, anywhere, scalars, scalars],
        out_specs=pl.BlockSpec(memory_space=vmem),
        scratch_shapes=[
            vmem((LEV, ROWS, COLS), F32),
            vmem((8, 2, LEV, ROWS, COLS), BF16),
            extended, extended, extended, extended,
            coefficient, coefficient, coefficient,
            vmem((XROWS, 8, COLS), F32),
            vmem((STEPS, XROWS, 8, COLS), F32),
            vmem((2, 4, 8, COLS), F32), vmem((2, 4, 8, COLS), F32),
            vmem((2, 6, 8, COLS), F32), vmem((2, 6, 8, COLS), F32),
            vmem((ROWS * LEV, COLS), F32),
            vmem((LEV, ROWS, COLS), F32),
            vmem((2, 16, ROWS + 2 * REACH, COLS), F32),
            vmem((16 * ROWS, COLS), F32),
            vmem((2, 32, COLS), F32), vmem((2, 32, COLS), F32),
            vmem((2, 32, COLS), F32), vmem((2, 32, COLS), F32),
            vmem((16 * ROWS, COLS), F32),
            vmem((2, 2 * COLS, COLS), BF16),
            vmem((16 * ROWS, COLS), F32),
            pltpu.SemaphoreType.DMA, pltpu.SemaphoreType.DMA,
            dma(len(FLOWS), CHUNKS), dma(len(FLOWS), CHUNKS),
            dma(2, 8), dma(2, 8),
            dma(2, 8, 2), dma(2, 8, 2),
            dma(2, 2), dma(2, 2),
        ],
        compiler_params=pltpu.CompilerParams(collective_id=0, has_side_effects=True),
        name="ensemble_step",
    )(residual_in, members, wind_x, wind_y)
    return (analysis, residual_in - relax * analysis)


def solution(mesh):
    return jax.shard_map(
        functools.partial(per_device, mesh.shape["tile"], mesh.shape["member"]),
        mesh=mesh,
        in_specs=(P(None, "tile", "member"), P("member", None, "tile", None), P(), P()),
        out_specs=(P(None, "tile", "member"), P(None, "tile", "member")),
        check_vma=False,
    )
```

time: 562 us -> 103 us (0.18)
  waiting for transfers between devices: 364 us -> 0 us
  starting transfers between devices: 133 us -> 0 us
  Pallas kernels: 0 us -> 97.8 us
  other arithmetic: 29.6 us -> 1.9 us
  between operations: 14.5 us -> 0.65 us
  local copies, waits for them, and re-layouts: 15.3 us -> 1.87 us
    psum x2 -> x0, waiting for transfers between devices: 217 us -> none  [per_device(): summed = lax.psum(partial_sum, 'member')]
    ppermute x36 -> x0, starting transfers between devices: 133 us -> none  [the longest x18 89.6 us: padded_2(): lax.ppermute(lax.slice_in_dim(block, block.shape[dim] - width, None, axis...]
    all_gather x2 -> x0, waiting for transfers between devices: 117 us -> none  [per_device(): lax.all_gather(grad, 'member', axis=2, tiled=True).astype(jnp.float32)]
    pallas_call x0 -> x1, Pallas kernels: none -> 97.8 us  [per_device(): pl.pallas_call(functools.partial(kernel, tiles, blocks), out_shape=jax.Sh...]
    ppermute x36 -> x0, waiting for transfers between devices: 30.5 us -> none  [the longest x18 24.8 us: padded_2(): lax.ppermute(lax.slice_in_dim(block, 0, width, axis=dim), axis, backward)]
    reduce_sum x4 -> x0, other arithmetic: 8.65 us -> none  [the longest x2 6.4 us: per_device(): partial_sum = jnp.sum(members_f * localized[:, None], axis=0)]
    slice x32 -> x0, local copies, waits for them, and re-layouts: 8.48 us -> none  [the longest x16 4.59 us: padded_2(): lax.slice_in_dim(block, 0, width, axis=dim)]
    convert_element_type x4 -> x0, other arithmetic: 7.43 us -> none  [the longest x2 4.46 us: per_device(): lax.all_gather(grad, 'member', axis=2, tiled=True).astype(jnp.float32)]
  transfers between devices with their start and end apart: 40 -> 0, of which waited for: 24 -> 0; matrix products, arithmetic and copies ran while one was open for 1% -> 0% of each run, Pallas kernels for 0% -> 0%
where the time goes in v1:
time: 103 us; the launch traced here: 102 us
  Pallas kernels  97.8 us (95%)
  other arithmetic  1.9 us (2%)
  local copies, waits for them, and re-layouts  1.87 us (2%)
    pallas_call x1, Pallas kernels, per_device(): pl.pallas_call(functools.partial(kernel, tiles, blocks), out_shape=jax.Sh...  97.8 us

profile of v1, /device:TPU:29, one launch (start us, length us, event | category | flops | bytes accessed | tf_op | source)
XLA Modules:
  0.0 102.2 jit_solution(4695531575424820406)
XLA Ops:
  0.6 0.0 copy-start
  0.6 97.8 %ensemble_step.1 = f32[64,16,128]{2,1,0:T(8,128)} custom-call(f32[64,16,128]{2,1,0:T(8,128)} %res_hbm.1, bf16[2,64,16,1024]{3,2,1,0:T(8,128)(2,1)} %mem_hbm.1, f32[64]{0:T(128)} %wx_ref.1, f32[64]{0:T(128)} %wy_ref.1), custom_call_target="tpu_custom_call" | custom-call | tf_op jit(solution)/shard_map/ensemble_step/pallas_call | solution.py:482
  98.5 0.0 copy-done
  98.5 1.9 %multiply_subtract_fusion = f32[64,16,128]{2,1,0:T(8,128)} fusion(f32[64,16,128]{2,1,0:T(8,128)S(1)} %copy-done, f32[64,16,128]{2,1,0:T(8,128)} %ensemble_step.1), kind=kLoop, calls=%fused_computation | loop fusion | flops 262144 | bytes 1572864 | tf_op jit(solution)/shard_map/sub | solution.py:514
  100.4 1.9 %copy.7 = f32[64,16,128]{2,1,0:T(8,128)} copy(f32[64,16,128]{2,1,0:T(8,128)} %ensemble_step.1) | data formatting | bytes 1048576
Async XLA Ops:
  0.6 97.8 %copy-start = (f32[64,16,128]{2,1,0:T(8,128)S(1)}, f32[64,16,128]{2,1,0:T(8,128)}, u32[]{:S(2)}) copy-start(f32[64,16,128]{2,1,0:T(8,128)} %res_hbm.1) | copy-start | bytes 1572868

commit v2 on v1

--- a/solution.py
+++ b/solution.py
@@ -19,7 +19,7 @@
 HALO = STEPS
 XROWS = ROWS + 2 * HALO
 REACH = 16
-CHUNKS = 4
+CHUNKS = 8
 CLEV = LEV // CHUNKS
 
 diffusion = 0.1
@@ -38,7 +38,7 @@
 def kernel(
     tiles, blocks,
     res_hbm, mem_hbm, wx_ref, wy_ref,
-    ana_ref,
+    out_ref,
     res, mt, a0, a1, w1, w2, c0, ax, ay, own, strip, mr, ml, ql, qr, gt, g,
     proj, sx, pk_r, pk_l, cl, cr, hx, band, z,
     own_sem, res_sem, m_send, m_recv, h_send, h_recv, p_send, p_recv, c_send, c_recv,
@@ -177,7 +177,7 @@
             own[HALO + r] = edges(a, HALO + r)
             return carry
 
-        lax.fori_loop(0, ROWS, pack, 0)
+        lax.fori_loop(0, ROWS, pack, 0, unroll=8 if it else 2)
         for quad in range(4):
             right = jnp.zeros((8, COLS), F32)
             left = jnp.zeros((8, COLS), F32)
@@ -249,7 +249,7 @@
             own[r + HALO + ROWS] = edges(a, r + HALO + ROWS)
             return carry
 
-        lax.fori_loop(0, HALO, pack, 0)
+        lax.fori_loop(0, HALO, pack, 0, unroll=HALO if it else 1)
         for r in range(XROWS):
             left = pltpu.roll(ql[it, r // 4], (-4 * (r % 4)) % COLS, 1)
             right = pltpu.roll(qr[it, r // 4], (12 - 4 * (r % 4)) % COLS, 1)
@@ -301,11 +301,14 @@
                 return carry
 
             if step < STEPS:
-                lax.fori_loop(step, HALO, functools.partial(row, scale=row_low), 0)
-            lax.fori_loop(HALO, HALO + ROWS, row, 0)
+                lax.fori_loop(
+                    step, HALO, functools.partial(row, scale=row_low), 0, unroll=True if it else 1
+                )
+            lax.fori_loop(HALO, HALO + ROWS, row, 0, unroll=ROWS if it else 2)
             if step < STEPS:
                 lax.fori_loop(
-                    HALO + ROWS, XROWS - step, functools.partial(row, scale=row_high), 0
+                    HALO + ROWS, XROWS - step, functools.partial(row, scale=row_high), 0,
+                    unroll=True if it else 1,
                 )
 
         def gather(l, carry):
@@ -424,12 +427,13 @@
             for i in range(width):
                 l = width * step + i
                 if it == 0:
-                    ana_ref[l] = sums[i]
-                    v = res[l] - relax * sums[i]
+                    half = relax * sums[i]
+                    out_ref[l] = half
+                    v = res[l] - half
                     a1[pl.ds(HALO * LEV + l, 8, stride=LEV), :] = v[0:8]
                     a1[pl.ds((HALO + 8) * LEV + l, 8, stride=LEV), :] = v[8:16]
                 else:
-                    ana_ref[l] = ana_ref[l] + sums[i]
+                    out_ref[l] = out_ref[l] + relax * sums[i]
             return carry
 
         lax.fori_loop(0, LEV // width, levels, 0)
@@ -479,7 +483,7 @@
     scalars = pl.BlockSpec(memory_space=pltpu.SMEM)
     extended = vmem((XROWS * LEV, COLS), F32)
     coefficient = vmem((LEV, COLS), F32)
-    analysis = pl.pallas_call(
+    half = pl.pallas_call(
         functools.partial(kernel, tiles, blocks),
         out_shape=jax.ShapeDtypeStruct((LEV, ROWS, COLS), F32),
         in_specs=[anywhere, anywhere, scalars, scalars],
@@ -511,7 +515,7 @@
         compiler_params=pltpu.CompilerParams(collective_id=0, has_side_effects=True),
         name="ensemble_step",
     )(residual_in, members, wind_x, wind_y)
-    return (analysis, residual_in - relax * analysis)
+    return (half * (1.0 / relax), residual_in - half)
 
 
 def solution(mesh):

time: 103 us -> 92.6 us (0.90)
  Pallas kernels: 97.8 us -> 89.7 us
  local copies, waits for them, and re-layouts: 1.87 us -> 0.01 us
    pallas_call x1, Pallas kernels: 97.8 us -> 89.7 us  [per_device(): pl.pallas_call(functools.partial(kernel, tiles, blocks), out_shape=jax.Sh...]
    unnamed x3 -> x2, local copies, waits for them, and re-layouts: 1.87 us -> 0.01 us
where the time goes in v2:
time: 92.6 us; the launch traced here: 92.5 us
  Pallas kernels  89.7 us (97%)
  other arithmetic  2.08 us (2%)
    pallas_call x1, Pallas kernels, per_device(): pl.pallas_call(functools.partial(kernel, tiles, blocks), out_shape=jax.Sh...  89.7 us
    sub x1, other arithmetic, per_device(): return (half * (1.0 / relax), residual_in - half)  2.08 us

profile of v2, /device:TPU:29, one launch (start us, length us, event | category | flops | bytes accessed | tf_op | source)
XLA Modules:
  0.0 92.5 jit_solution(205431369290706216)
XLA Ops:
  0.6 0.0 copy-start
  0.6 89.7 %ensemble_step.1 = f32[64,16,128]{2,1,0:T(8,128)} custom-call(f32[64,16,128]{2,1,0:T(8,128)} %res_hbm.1, bf16[2,64,16,1024]{3,2,1,0:T(8,128)(2,1)} %mem_hbm.1, f32[64]{0:T(128)} %wx_ref.1, f32[64]{0:T(128)} %wy_ref.1), custom_call_target="tpu_custom_call" | custom-call | tf_op jit(solution)/shard_map/ensemble_step/pallas_call | solution.py:486
  90.4 0.0 copy-done
  90.4 2.1 %fusion = (f32[64,16,128]{2,1,0:T(8,128)}, f32[64,16,128]{2,1,0:T(8,128)}) fusion(f32[64,16,128]{2,1,0:T(8,128)S(1)} %copy-done, f32[64,16,128]{2,1,0:T(8,128)} %ensemble_step.1), kind=kLoop, calls=%fused_computation.1 | loop fusion | flops 262144 | bytes 2097152 | tf_op jit(solution)/shard_map/sub | solution.py:518
Async XLA Ops:
  0.6 89.7 %copy-start = (f32[64,16,128]{2,1,0:T(8,128)S(1)}, f32[64,16,128]{2,1,0:T(8,128)}, u32[]{:S(2)}) copy-start(f32[64,16,128]{2,1,0:T(8,128)} %res_hbm.1) | copy-start | bytes 1572868

commit v3 on v2

--- a/solution.py
+++ b/solution.py
@@ -25,8 +25,11 @@
 diffusion = 0.1
 relax = 0.5
 
-FLOWS = ((2, 1), (1, 1), (3, 1), (0, 1), (2, 0), (1, 0), (3, 0))
+FLOWS = ((1, 1), (3, 1), (0, 1), (2, 1), (1, 0), (3, 0), (2, 0))
 SIDES = ((1, 0), (-1, 0), (0, 1), (0, -1), (1, 1), (-1, 1), (1, -1), (-1, -1))
+
+
+COLUMN_SIDES = ((1, 1), (-1, 1), (1, -1), (-1, -1), (0, 1), (0, -1))
 
 
 def taper_weights():
@@ -37,11 +40,11 @@
 
 def kernel(
     tiles, blocks,
-    res_hbm, mem_hbm, wx_ref, wy_ref,
+    res_hbm, mem_hbm, wx_hbm, wy_hbm,
     out_ref,
-    res, mt, a0, a1, w1, w2, c0, ax, ay, own, strip, mr, ml, ql, qr, gt, g,
+    res, mt, a0, a1, w1, w2, c0, ax, ay, own, strip, sides, mr, ml, ql, qr, gt, g,
     proj, sx, pk_r, pk_l, cl, cr, hx, band, z,
-    own_sem, res_sem, m_send, m_recv, h_send, h_recv, p_send, p_recv, c_send, c_recv,
+    wx_ref, wy_ref, own_sem, res_sem, wind_sem, m_send, m_recv, h_send, h_recv, p_send, p_recv, c_send, c_recv,
 ):
     t = lax.axis_index("tile")
     m = lax.axis_index("member")
@@ -64,6 +67,12 @@
 
     res_copy = pltpu.make_async_copy(res_hbm, res, res_sem)
     res_copy.start()
+    wind_copies = [
+        pltpu.make_async_copy(wind, wind_ref, wind_sem.at[n])
+        for n, (wind, wind_ref) in enumerate(((wx_hbm, wx_ref), (wy_hbm, wy_ref)))
+    ]
+    for copy in wind_copies:
+        copy.start()
     own_copy = pltpu.make_async_copy(
         mem_hbm.at[:, :, :, pl.ds(pl.multiple_of(m * COLS, COLS), COLS)], mt.at[m], own_sem
     )
@@ -109,6 +118,8 @@
         ql[:, 0] = jnp.zeros((2, 8, COLS), F32)
         qr[:, 0] = jnp.zeros((2, 8, COLS), F32)
         proj[:, :, 0:REACH, :] = jnp.zeros((2, 16, REACH, COLS), F32)
+        cl[:, :, 0:REACH, :] = jnp.zeros((2, 2, REACH, COLS), F32)
+        cr[:, :, 0:REACH, :] = jnp.zeros((2, 2, REACH, COLS), F32)
 
     @pl.when(t == tiles - 1)
     def _():
@@ -117,6 +128,8 @@
         ql[:, 5] = jnp.zeros((2, 8, COLS), F32)
         qr[:, 5] = jnp.zeros((2, 8, COLS), F32)
         proj[:, :, REACH + ROWS :, :] = jnp.zeros((2, 16, REACH, COLS), F32)
+        cl[:, :, REACH + ROWS :, :] = jnp.zeros((2, 2, REACH, COLS), F32)
+        cr[:, :, REACH + ROWS :, :] = jnp.zeros((2, 2, REACH, COLS), F32)
 
     @pl.when(m == 0)
     def _():
@@ -204,6 +217,9 @@
     for c in range(1, CHUNKS):
         for i in range(len(FLOWS)):
             member_copy(i, c).start()
+
+    for copy in wind_copies:
+        copy.wait()
 
     def coefficients(l, carry):
         wx, wy = wx_ref[l], wy_ref[l]
@@ -269,26 +285,27 @@
                 elif r >= HALO + ROWS:
                     out = out * row_high
                 strip[step, r] = out
+        for step in range(STEPS):
+            for r in range(step + 1, XROWS - step - 1):
+                v = strip[step, r]
+                sides[step, r] = jnp.where(
+                    q == 0, pltpu.roll(v, COLS - 12, 1), pltpu.roll(v, COLS - 2, 1)
+                )
         for step in range(1, STEPS + 1):
             src = (a, w1, w2, w1)[step - 1]
             dst = (w1, w2, w1, gt)[step - 1]
 
             def row(r, carry, scale=None):
-                side = strip[step - 1, r]
+                side = sides[step - 1, r]
                 for k in range(GROUPS):
                     at = r * LEV + 8 * k
                     here = pl.ds(pl.multiple_of(at, 8), 8)
                     v = src[here, :]
                     up = src[pl.ds(pl.multiple_of(at - LEV, 8), 8), :]
                     down = src[pl.ds(pl.multiple_of(at + LEV, 8), 8), :]
-                    left = jnp.where(
-                        lane == 0, pltpu.roll(side, (-(16 * k + 3)) % COLS, 1), pltpu.roll(v, 1, 1)
-                    )
-                    right = jnp.where(
-                        lane == COLS - 1,
-                        pltpu.roll(side, (COLS - 1 - (16 * k + 12)) % COLS, 1),
-                        pltpu.roll(v, COLS - 1, 1),
-                    )
+                    ends = pltpu.roll(side, COLS - 1 - 16 * k, 1)
+                    left = jnp.where(lane == 0, ends, pltpu.roll(v, 1, 1))
+                    right = jnp.where(lane == COLS - 1, ends, pltpu.roll(v, COLS - 1, 1))
                     s = slice(8 * k, 8 * k + 8)
                     out = c0[s, :] * v + (up + left) + ax[s, :] * down + ay[s, :] * right
                     if scale is not None:
@@ -348,6 +365,15 @@
         for d in (0, 1):
             guarded(there(*SIDES[d]), project_copy(it, pairs[slot], slot, d).start)
 
+    def taper(ref, lead, at):
+        total = w[REACH] * ref[(*lead, pl.ds(at, 8), slice(None))]
+        for k in range(1, REACH + 1):
+            total = total + w[REACH + k] * (
+                ref[(*lead, pl.ds(at - k, 8), slice(None))]
+                + ref[(*lead, pl.ds(at + k, 8), slice(None))]
+            )
+        return total
+
     def smooth_rows(it, slot):
         pair = pairs[slot]
         for d in (0, 1):
@@ -355,21 +381,33 @@
             guarded(there(-dt, -dm), project_copy(it, pair, slot, d).wait_recv)
         for n in range(2):
             for half in (0, 8):
-                at = REACH + half
-                total = w[REACH] * proj[it, 2 * pair + n, pl.ds(at, 8), :]
-                for k in range(1, REACH + 1):
-                    total = total + w[REACH + k] * (
-                        proj[it, 2 * pair + n, pl.ds(at - k, 8), :]
-                        + proj[it, 2 * pair + n, pl.ds(at + k, 8), :]
-                    )
-                sx[pl.ds(pl.multiple_of((2 * pair + n) * ROWS + half, 8), 8), :] = total
+                sx[pl.ds(pl.multiple_of((2 * pair + n) * ROWS + half, 8), 8), :] = taper(
+                    proj, (it, 2 * pair + n), REACH + half
+                )
 
     def column_copy(it, d):
-        src, dst = (pk_r.at[it], cl.at[it]) if d == 0 else (pk_l.at[it], cr.at[it])
+        dt, dm = COLUMN_SIDES[d]
+        src, dst = (pk_r.at[it], cl.at[it]) if dm > 0 else (pk_l.at[it], cr.at[it])
         return pltpu.make_async_remote_copy(
-            src_ref=src, dst_ref=dst, send_sem=c_send.at[it, d], recv_sem=c_recv.at[it, d],
-            device_id=peer(0, 1 if d == 0 else -1), device_id_type=MESH,
+            src_ref=src,
+            dst_ref=dst.at[:, pl.ds(REACH if dt == 0 else 0 if dt > 0 else REACH + ROWS, ROWS)],
+            send_sem=c_send.at[it, d], recv_sem=c_recv.at[it, d],
+            device_id=peer(dt, dm), device_id_type=MESH,
         )
+
+    def send_columns(it):
+        for part in range(2):
+            for half in (0, 8):
+                right = jnp.zeros((8, COLS), F32)
+                left = jnp.zeros((8, COLS), F32)
+                for n in range(8):
+                    v = proj[it, 8 * part + n, REACH + half : REACH + half + 8, :]
+                    right = jnp.where(group == n, pltpu.roll(v, (16 * n - 112) % COLS, 1), right)
+                    left = jnp.where(group == n, pltpu.roll(v, 16 * n, 1), left)
+                pk_r[it, part, half : half + 8, :] = right
+                pk_l[it, part, half : half + 8, :] = left
+        for d, side in enumerate(COLUMN_SIDES):
+            guarded(there(*side), column_copy(it, d).start)
 
     def split(x):
         high = x.astype(BF16)
@@ -383,28 +421,13 @@
         return dot(high, b_high) + (dot(low, b_high) + dot(high, b_low))
 
     def smooth_columns(it):
+        z[...] = times(sx[...], 0)
+        for d, (dt, dm) in enumerate(COLUMN_SIDES):
+            guarded(there(-dt, -dm), column_copy(it, d).wait_recv)
         for part in range(2):
             for half in (0, 8):
-                right = jnp.zeros((8, COLS), F32)
-                left = jnp.zeros((8, COLS), F32)
-                for n in range(8):
-                    at = (8 * part + n) * ROWS + half
-                    v = sx[at : at + 8, :]
-                    right = jnp.where(group == n, pltpu.roll(v, (16 * n - 112) % COLS, 1), right)
-                    left = jnp.where(group == n, pltpu.roll(v, 16 * n, 1), left)
-                at = part * ROWS + half
-                pk_r[it, at : at + 8, :] = right
-                pk_l[it, at : at + 8, :] = left
-        guarded(there(0, 1), column_copy(it, 0).start)
-        guarded(there(0, -1), column_copy(it, 1).start)
-        z[...] = times(sx[...], 0)
-        guarded(there(0, -1), column_copy(it, 0).wait_recv)
-        guarded(there(0, 1), column_copy(it, 1).wait_recv)
-        for part in range(2):
-            for half in (0, 8):
-                at = part * ROWS + half
-                from_left = cl[it, at : at + 8, :]
-                from_right = cr[it, at : at + 8, :]
+                from_left = taper(cl, (it, part), REACH + half)
+                from_right = taper(cr, (it, part), REACH + half)
                 for n in range(8):
                     to = (8 * part + n) * ROWS + half
                     hx[to : to + 8, :] = jnp.where(
@@ -448,6 +471,7 @@
             project(0, pairs[1 + i], c * CLEV, CLEV, c == 0)
             if c == CHUNKS - 1:
                 send_project(0, 1 + i)
+    send_columns(0)
     for slot in range(8):
         smooth_rows(0, slot)
     smooth_columns(0)
@@ -458,6 +482,7 @@
     for slot in range(8):
         project(1, pairs[slot], 0, LEV, True)
         send_project(1, slot)
+    send_columns(1)
     for slot in range(8):
         smooth_rows(1, slot)
     smooth_columns(1)
@@ -472,21 +497,20 @@
         for slot in range(8):
             for d in (0, 1):
                 guarded(there(*SIDES[d]), project_copy(it, pairs[slot], slot, d).wait_send)
-        guarded(there(0, 1), column_copy(it, 0).wait_send)
-        guarded(there(0, -1), column_copy(it, 1).wait_send)
+        for d, side in enumerate(COLUMN_SIDES):
+            guarded(there(*side), column_copy(it, d).wait_send)
 
 
 def per_device(tiles, blocks, residual_in, members, wind_x, wind_y):
     vmem = pltpu.VMEM
     dma = lambda *shape: pltpu.SemaphoreType.DMA(shape)
     anywhere = pl.BlockSpec(memory_space=pl.ANY)
-    scalars = pl.BlockSpec(memory_space=pltpu.SMEM)
     extended = vmem((XROWS * LEV, COLS), F32)
     coefficient = vmem((LEV, COLS), F32)
     half = pl.pallas_call(
         functools.partial(kernel, tiles, blocks),
         out_shape=jax.ShapeDtypeStruct((LEV, ROWS, COLS), F32),
-        in_specs=[anywhere, anywhere, scalars, scalars],
+        in_specs=[anywhere] * 4,
         out_specs=pl.BlockSpec(memory_space=vmem),
         scratch_shapes=[
             vmem((LEV, ROWS, COLS), F32),
@@ -495,22 +519,25 @@
             coefficient, coefficient, coefficient,
             vmem((XROWS, 8, COLS), F32),
             vmem((STEPS, XROWS, 8, COLS), F32),
+            vmem((STEPS, XROWS, 8, COLS), F32),
             vmem((2, 4, 8, COLS), F32), vmem((2, 4, 8, COLS), F32),
             vmem((2, 6, 8, COLS), F32), vmem((2, 6, 8, COLS), F32),
             vmem((ROWS * LEV, COLS), F32),
             vmem((LEV, ROWS, COLS), F32),
             vmem((2, 16, ROWS + 2 * REACH, COLS), F32),
             vmem((16 * ROWS, COLS), F32),
-            vmem((2, 32, COLS), F32), vmem((2, 32, COLS), F32),
-            vmem((2, 32, COLS), F32), vmem((2, 32, COLS), F32),
+            vmem((2, 2, ROWS, COLS), F32), vmem((2, 2, ROWS, COLS), F32),
+            vmem((2, 2, ROWS + 2 * REACH, COLS), F32),
+            vmem((2, 2, ROWS + 2 * REACH, COLS), F32),
             vmem((16 * ROWS, COLS), F32),
             vmem((2, 2 * COLS, COLS), BF16),
             vmem((16 * ROWS, COLS), F32),
-            pltpu.SemaphoreType.DMA, pltpu.SemaphoreType.DMA,
+            pltpu.SMEM((LEV,), F32), pltpu.SMEM((LEV,), F32),
+            pltpu.SemaphoreType.DMA, pltpu.SemaphoreType.DMA, dma(2),
             dma(len(FLOWS), CHUNKS), dma(len(FLOWS), CHUNKS),
             dma(2, 8), dma(2, 8),
             dma(2, 8, 2), dma(2, 8, 2),
-            dma(2, 2), dma(2, 2),
+            dma(2, len(COLUMN_SIDES)), dma(2, len(COLUMN_SIDES)),
         ],
         compiler_params=pltpu.CompilerParams(collective_id=0, has_side_effects=True),
         name="ensemble_step",

time: 92.6 us -> 87.7 us (0.947)
  Pallas kernels: 89.7 us -> 84.3 us
    pallas_call x1, Pallas kernels: 89.7 us -> 84.3 us  [per_device(): pl.pallas_call(functools.partial(kernel, tiles, blocks), out_shape=jax.Sh...]
where the time goes in v3:
time: 87.7 us; the launch traced here: 87 us
  Pallas kernels  84.3 us (96%)
  other arithmetic  2.08 us (2%)
    pallas_call x1, Pallas kernels, per_device(): pl.pallas_call(functools.partial(kernel, tiles, blocks), out_shape=jax.Sh...  84.3 us
    sub x1, other arithmetic, per_device(): return (half * (1.0 / relax), residual_in - half)  2.08 us

profile of v3, /device:TPU:29, one launch (start us, length us, event | category | flops | bytes accessed | tf_op | source)
XLA Modules:
  0.0 87.0 jit_solution(3231059017774697500)
XLA Ops:
  0.6 0.0 copy-start
  0.6 84.3 %ensemble_step.1 = f32[64,16,128]{2,1,0:T(8,128)} custom-call(f32[64,16,128]{2,1,0:T(8,128)} %res_hbm.1, bf16[2,64,16,1024]{3,2,1,0:T(8,128)(2,1)} %mem_hbm.1, f32[64]{0:T(128)} %wx_hbm.1, f32[64]{0:T(128)} %wy_hbm.1), custom_call_target="tpu_custom_call" | custom-call | tf_op jit(solution)/shard_map/ensemble_step/pallas_call | solution.py:510
  84.9 0.0 copy-done
  84.9 2.1 %fusion = (f32[64,16,128]{2,1,0:T(8,128)}, f32[64,16,128]{2,1,0:T(8,128)}) fusion(f32[64,16,128]{2,1,0:T(8,128)S(1)} %copy-done, f32[64,16,128]{2,1,0:T(8,128)} %ensemble_step.1), kind=kLoop, calls=%fused_computation.1 | loop fusion | flops 262144 | bytes 2097152 | tf_op jit(solution)/shard_map/sub | solution.py:545
Async XLA Ops:
  0.6 84.3 %copy-start = (f32[64,16,128]{2,1,0:T(8,128)S(1)}, f32[64,16,128]{2,1,0:T(8,128)}, u32[]{:S(2)}) copy-start(f32[64,16,128]{2,1,0:T(8,128)} %res_hbm.1) | copy-start | bytes 1572868

commit v4 on v3

--- a/solution.py
+++ b/solution.py
@@ -25,7 +25,12 @@
 diffusion = 0.1
 relax = 0.5
 
-FLOWS = ((1, 1), (3, 1), (0, 1), (2, 1), (1, 0), (3, 0), (2, 0))
+FLOWS = ((2, 1), (0, 1), (2, 0), (1, 1), (3, 1), (1, 0), (3, 0))
+ORDER = [(i, c) for c in range(CHUNKS) for i in (0, 1, 2)]
+ORDER += [(i, c) for c in range(CHUNKS) for i in (3, 4, 5, 6)]
+FIRST = 6
+HALVES = 2
+HLEV = LEV // HALVES
 SIDES = ((1, 0), (-1, 0), (0, 1), (0, -1), (1, 1), (-1, 1), (1, -1), (-1, -1))
 
 
@@ -43,8 +48,8 @@
     res_hbm, mem_hbm, wx_hbm, wy_hbm,
     out_ref,
     res, mt, a0, a1, w1, w2, c0, ax, ay, own, strip, sides, mr, ml, ql, qr, gt, g,
-    proj, sx, pk_r, pk_l, cl, cr, hx, band, z,
-    wx_ref, wy_ref, own_sem, res_sem, wind_sem, m_send, m_recv, h_send, h_recv, p_send, p_recv, c_send, c_recv,
+    row_out, row_in, proj, proj_out, proj_in, sx, pk_r, pk_l, cl, cr, band, z,
+    wx_ref, wy_ref, own_sem, res_sem, wind_sem, m_send, m_recv, h_send, h_recv, r_send, r_recv, p_send, p_recv, c_send, c_recv,
 ):
     t = lax.axis_index("tile")
     m = lax.axis_index("member")
@@ -108,8 +113,8 @@
             device_id_type=MESH,
         )
 
-    for i in range(len(FLOWS)):
-        member_copy(i, 0).start()
+    for i, c in ORDER[:FIRST]:
+        member_copy(i, c).start()
 
     @pl.when(t == 0)
     def _():
@@ -145,21 +150,47 @@
     q = lane % 16
     group = lane // 16
 
+    def row_copy(it, d, half):
+        return pltpu.make_async_remote_copy(
+            src_ref=row_out.at[it, d, half], dst_ref=row_in.at[it, d, half],
+            send_sem=r_send.at[it, d, half], recv_sem=r_recv.at[it, d, half],
+            device_id=peer(*SIDES[d]), device_id_type=MESH,
+        )
+
+    def send_rows(it, half):
+        a = (a0, a1)[it]
+        for d, first in ((0, ROWS), (1, HALO)):
+            for r in range(HALO):
+                row_out[it, d, half, r * HLEV : (r + 1) * HLEV, :] = a[
+                    (first + r) * LEV + half * HLEV : (first + r) * LEV + (half + 1) * HLEV, :
+                ].astype(BF16)
+            guarded(there(*SIDES[d]), row_copy(it, d, half).start)
+
+    def receive_rows(it):
+        a = (a0, a1)[it]
+        for d, first in ((0, 0), (1, HALO + ROWS)):
+
+            def unpack(d=d, first=first):
+                for half in range(HALVES):
+                    row_copy(it, d, half).wait_recv()
+                    for r in range(HALO):
+                        at = (first + r) * LEV + half * HLEV
+                        a[at : at + HLEV, :] = row_in[
+                            it, d, half, r * HLEV : (r + 1) * HLEV, :
+                        ].astype(F32)
+
+            dt, dm = SIDES[d]
+            guarded(there(-dt, -dm), unpack)
+
     def quad_copy(it, d):
-        a = (a0, a1)[it]
         dt, dm = SIDES[d]
-        if dm == 0:
-            rows = HALO * LEV
-            src = a.at[pl.ds(ROWS * LEV if dt > 0 else HALO * LEV, rows)]
-            dst = a.at[pl.ds(0 if dt > 0 else (HALO + ROWS) * LEV, rows)]
+        src, dst = (mr.at[it], ql.at[it]) if dm > 0 else (ml.at[it], qr.at[it])
+        if dt == 0:
+            src, dst = src, dst.at[pl.ds(1, 4)]
+        elif dt > 0:
+            src, dst = src.at[pl.ds(3, 1)], dst.at[pl.ds(0, 1)]
         else:
-            src, dst = (mr.at[it], ql.at[it]) if dm > 0 else (ml.at[it], qr.at[it])
-            if dt == 0:
-                src, dst = src, dst.at[pl.ds(1, 4)]
-            elif dt > 0:
-                src, dst = src.at[pl.ds(3, 1)], dst.at[pl.ds(0, 1)]
-            else:
-                src, dst = src.at[pl.ds(0, 1)], dst.at[pl.ds(5, 1)]
+            src, dst = src.at[pl.ds(0, 1)], dst.at[pl.ds(5, 1)]
         return pltpu.make_async_remote_copy(
             src_ref=src, dst_ref=dst, send_sem=h_send.at[it, d], recv_sem=h_recv.at[it, d],
             device_id=peer(dt, dm), device_id_type=MESH,
@@ -183,8 +214,6 @@
 
     def send_halos(it):
         a = (a0, a1)[it]
-        for d in (0, 1):
-            guarded(there(*SIDES[d]), quad_copy(it, d).start)
 
         def pack(r, carry):
             own[HALO + r] = edges(a, HALO + r)
@@ -213,10 +242,11 @@
         return carry
 
     lax.fori_loop(0, LEV, spread, 0, unroll=4)
+    for half in range(HALVES):
+        send_rows(0, half)
     send_halos(0)
-    for c in range(1, CHUNKS):
-        for i in range(len(FLOWS)):
-            member_copy(i, c).start()
+    for i, c in ORDER[FIRST:]:
+        member_copy(i, c).start()
 
     for copy in wind_copies:
         copy.wait()
@@ -230,16 +260,23 @@
 
     lax.fori_loop(0, LEV, coefficients, 0)
 
-    j = lax.broadcasted_iota(jnp.int32, (2 * COLS, COLS), 0)
-    k = jnp.where(j < COLS + COLS // 2, j, j - 2 * COLS) - lax.broadcasted_iota(
-        jnp.int32, (2 * COLS, COLS), 1
-    )
     total_w = sum(1.0 - (i / 17.0) ** 2 for i in range(-16, 17))
-    kf = k.astype(F32)
-    full = jnp.where(jnp.abs(k) <= REACH, (1.0 - kf * kf * (1.0 / 289.0)) * (1.0 / total_w), 0.0)
-    coarse = full.astype(BF16)
-    band[0] = coarse
-    band[1] = (full - coarse.astype(F32)).astype(BF16)
+    source = lax.broadcasted_iota(jnp.int32, (COLS, COLS), 0)
+    target = lax.broadcasted_iota(jnp.int32, (COLS, COLS), 1)
+    together = source // 16 == target // 16
+    for which, k, near in (
+        (0, source - target, None),
+        (1, source - 16 - target, together),
+        (2, source + 16 - target, together),
+    ):
+        kf = k.astype(F32)
+        reached = jnp.abs(k) <= REACH
+        if near is not None:
+            reached = jnp.logical_and(reached, near)
+        full = jnp.where(reached, (1.0 - kf * kf * (1.0 / 289.0)) * (1.0 / total_w), 0.0)
+        coarse = full.astype(BF16)
+        band[which, 0] = coarse
+        band[which, 1] = (full - coarse.astype(F32)).astype(BF16)
 
     def strip_coefficient(ref):
         total = jnp.zeros((8, COLS), F32)
@@ -256,7 +293,8 @@
 
     def adjoint(it):
         a = (a0, a1)[it]
-        for d in range(8):
+        receive_rows(it)
+        for d in range(2, 8):
             dt, dm = SIDES[d]
             guarded(there(-dt, -dm), quad_copy(it, d).wait_recv)
 
@@ -347,14 +385,14 @@
             v = g[l]
             return tuple(s + mt[pair, n, l].astype(F32) * v for n, s in enumerate(sums))
 
-        sums = lax.fori_loop(first, first + count, level, start, unroll=4)
+        sums = lax.fori_loop(first, first + count, level, start, unroll=8)
         for n in range(2):
             proj[it, 2 * pair + n, own_rows, :] = sums[n]
 
     def project_copy(it, pair, slot, d):
         return pltpu.make_async_remote_copy(
-            src_ref=proj.at[it, pl.ds(2 * pair, 2), own_rows],
-            dst_ref=proj.at[it, pl.ds(2 * pair, 2), pl.ds(0 if d == 0 else REACH + ROWS, REACH)],
+            src_ref=proj_out.at[it, pl.ds(2 * pair, 2)],
+            dst_ref=proj_in.at[it, d, pl.ds(2 * pair, 2)],
             send_sem=p_send.at[it, slot, d], recv_sem=p_recv.at[it, slot, d],
             device_id=peer(*SIDES[d]), device_id_type=MESH,
         )
@@ -362,6 +400,9 @@
     pairs = [m] + [mate(-dy, dz) for dy, dz in FLOWS]
 
     def send_project(it, slot):
+        for n in range(2):
+            member = 2 * pairs[slot] + n
+            proj_out[it, member] = proj[it, member, own_rows, :].astype(BF16)
         for d in (0, 1):
             guarded(there(*SIDES[d]), project_copy(it, pairs[slot], slot, d).start)
 
@@ -377,8 +418,16 @@
     def smooth_rows(it, slot):
         pair = pairs[slot]
         for d in (0, 1):
+
+            def unpack(d=d):
+                project_copy(it, pair, slot, d).wait_recv()
+                for n in range(2):
+                    proj[it, 2 * pair + n, pl.ds(0 if d == 0 else REACH + ROWS, REACH), :] = proj_in[
+                        it, d, 2 * pair + n
+                    ].astype(F32)
+
             dt, dm = SIDES[d]
-            guarded(there(-dt, -dm), project_copy(it, pair, slot, d).wait_recv)
+            guarded(there(-dt, -dm), unpack)
         for n in range(2):
             for half in (0, 8):
                 sx[pl.ds(pl.multiple_of((2 * pair + n) * ROWS + half, 8), 8), :] = taper(
@@ -413,32 +462,37 @@
         high = x.astype(BF16)
         return high, (x - high.astype(F32)).astype(BF16)
 
-    def times(x, part):
+    def times(x, which):
         high, low = split(x)
-        rows = slice(part * COLS, part * COLS + COLS)
-        b_high, b_low = band[0, rows, :], band[1, rows, :]
         dot = functools.partial(jnp.dot, preferred_element_type=F32)
-        return dot(high, b_high) + (dot(low, b_high) + dot(high, b_low))
+        return dot(high, band[which, 0]) + (dot(low, band[which, 0]) + dot(high, band[which, 1]))
 
     def smooth_columns(it):
         z[...] = times(sx[...], 0)
         for d, (dt, dm) in enumerate(COLUMN_SIDES):
             guarded(there(-dt, -dm), column_copy(it, d).wait_recv)
+        outer = []
+        for which, ref in ((1, cl), (2, cr)):
+            x = jnp.concatenate(
+                [taper(ref, (it, part), REACH + half) for part in range(2) for half in (0, 8)]
+            )
+            outer.append(times(x, which))
         for part in range(2):
             for half in (0, 8):
-                from_left = taper(cl, (it, part), REACH + half)
-                from_right = taper(cr, (it, part), REACH + half)
+                at = part * ROWS + half
+                from_left, from_right = (x[at : at + 8, :] for x in outer)
                 for n in range(8):
                     to = (8 * part + n) * ROWS + half
-                    hx[to : to + 8, :] = jnp.where(
+                    z[to : to + 8, :] = z[to : to + 8, :] + jnp.where(
                         lane < 16,
-                        pltpu.roll(from_right, (-16 * n) % COLS, 1),
-                        jnp.where(lane >= 112, pltpu.roll(from_left, (112 - 16 * n) % COLS, 1), 0.0),
+                        pltpu.roll(from_left, (-16 * n) % COLS, 1),
+                        jnp.where(
+                            lane >= 112, pltpu.roll(from_right, (112 - 16 * n) % COLS, 1), 0.0
+                        ),
                     )
-        z[...] = z[...] + times(hx[...], 1)
 
     def increments(it):
-        width = 2
+        width = 4
 
         def levels(step, carry):
             sums = [jnp.zeros((ROWS, COLS), F32) for _ in range(width)]
@@ -459,18 +513,21 @@
                     out_ref[l] = out_ref[l] + relax * sums[i]
             return carry
 
-        lax.fori_loop(0, LEV // width, levels, 0)
+        for half in range(HALVES):
+            first = half * HLEV // width
+            lax.fori_loop(first, first + HLEV // width, levels, 0)
+            if it == 0:
+                send_rows(1, half)
 
     adjoint(0)
     own_copy.wait()
     project(0, pairs[0], 0, LEV, True)
     send_project(0, 0)
-    for c in range(CHUNKS):
-        for i in range(len(FLOWS)):
-            member_copy(i, c).wait_recv()
-            project(0, pairs[1 + i], c * CLEV, CLEV, c == 0)
-            if c == CHUNKS - 1:
-                send_project(0, 1 + i)
+    for i, c in ORDER:
+        member_copy(i, c).wait_recv()
+        project(0, pairs[1 + i], c * CLEV, CLEV, c == 0)
+        if c == CHUNKS - 1:
+            send_project(0, 1 + i)
     send_columns(0)
     for slot in range(8):
         smooth_rows(0, slot)
@@ -488,11 +545,13 @@
     smooth_columns(1)
     increments(1)
 
-    for c in range(CHUNKS):
-        for i in range(len(FLOWS)):
-            member_copy(i, c).wait_send()
+    for i, c in ORDER:
+        member_copy(i, c).wait_send()
     for it in range(2):
-        for d in range(8):
+        for d in (0, 1):
+            for half in range(HALVES):
+                guarded(there(*SIDES[d]), row_copy(it, d, half).wait_send)
+        for d in range(2, 8):
             guarded(there(*SIDES[d]), quad_copy(it, d).wait_send)
         for slot in range(8):
             for d in (0, 1):
@@ -524,18 +583,22 @@
             vmem((2, 6, 8, COLS), F32), vmem((2, 6, 8, COLS), F32),
             vmem((ROWS * LEV, COLS), F32),
             vmem((LEV, ROWS, COLS), F32),
+            vmem((2, 2, HALVES, HALO * HLEV, COLS), BF16),
+            vmem((2, 2, HALVES, HALO * HLEV, COLS), BF16),
             vmem((2, 16, ROWS + 2 * REACH, COLS), F32),
+            vmem((2, 16, ROWS, COLS), BF16),
+            vmem((2, 2, 16, REACH, COLS), BF16),
             vmem((16 * ROWS, COLS), F32),
             vmem((2, 2, ROWS, COLS), F32), vmem((2, 2, ROWS, COLS), F32),
             vmem((2, 2, ROWS + 2 * REACH, COLS), F32),
             vmem((2, 2, ROWS + 2 * REACH, COLS), F32),
-            vmem((16 * ROWS, COLS), F32),
-            vmem((2, 2 * COLS, COLS), BF16),
+            vmem((3, 2, COLS, COLS), BF16),
             vmem((16 * ROWS, COLS), F32),
             pltpu.SMEM((LEV,), F32), pltpu.SMEM((LEV,), F32),
             pltpu.SemaphoreType.DMA, pltpu.SemaphoreType.DMA, dma(2),
             dma(len(FLOWS), CHUNKS), dma(len(FLOWS), CHUNKS),
             dma(2, 8), dma(2, 8),
+            dma(2, 2, HALVES), dma(2, 2, HALVES),
             dma(2, 8, 2), dma(2, 8, 2),
             dma(2, len(COLUMN_SIDES)), dma(2, len(COLUMN_SIDES)),
         ],

time: 87.7 us -> 84.3 us (0.961)
  Pallas kernels: 84.3 us -> 81.4 us
    pallas_call x1, Pallas kernels: 84.3 us -> 81.4 us  [per_device(): pl.pallas_call(functools.partial(kernel, tiles, blocks), out_shape=jax.Sh...]
where the time goes in v4:
time: 84.3 us; the launch traced here: 84.2 us
  Pallas kernels  81.4 us (97%)
  other arithmetic  2.08 us (2%)
    pallas_call x1, Pallas kernels, per_device(): pl.pallas_call(functools.partial(kernel, tiles, blocks), out_shape=jax.Sh...  81.4 us
    sub x1, other arithmetic, per_device(): return (half * (1.0 / relax), residual_in - half)  2.08 us

profile of v4, /device:TPU:29, one launch (start us, length us, event | category | flops | bytes accessed | tf_op | source)
XLA Modules:
  0.0 84.2 jit_solution(343867480916222466)
XLA Ops:
  0.6 0.0 copy-start
  0.6 81.4 %ensemble_step.1 = f32[64,16,128]{2,1,0:T(8,128)} custom-call(f32[64,16,128]{2,1,0:T(8,128)} %res_hbm.1, bf16[2,64,16,1024]{3,2,1,0:T(8,128)(2,1)} %mem_hbm.1, f32[64]{0:T(128)} %wx_hbm.1, f32[64]{0:T(128)} %wy_hbm.1), custom_call_target="tpu_custom_call" | custom-call | tf_op jit(solution)/shard_map/ensemble_step/pallas_call | solution.py:569
  82.1 0.0 copy-done
  82.1 2.1 %fusion = (f32[64,16,128]{2,1,0:T(8,128)}, f32[64,16,128]{2,1,0:T(8,128)}) fusion(f32[64,16,128]{2,1,0:T(8,128)S(1)} %copy-done, f32[64,16,128]{2,1,0:T(8,128)} %ensemble_step.1), kind=kLoop, calls=%fused_computation.1 | loop fusion | flops 262144 | bytes 2097152 | tf_op jit(solution)/shard_map/sub | solution.py:608
Async XLA Ops:
  0.6 81.5 %copy-start = (f32[64,16,128]{2,1,0:T(8,128)S(1)}, f32[64,16,128]{2,1,0:T(8,128)}, u32[]{:S(2)}) copy-start(f32[64,16,128]{2,1,0:T(8,128)} %res_hbm.1) | copy-start | bytes 1572868

commit v5 on v4

--- a/solution.py
+++ b/solution.py
@@ -31,6 +31,7 @@
 FIRST = 6
 HALVES = 2
 HLEV = LEV // HALVES
+PARTS = 4
 SIDES = ((1, 0), (-1, 0), (0, 1), (0, -1), (1, 1), (-1, 1), (1, -1), (-1, -1))
 
 
@@ -46,10 +47,10 @@
 def kernel(
     tiles, blocks,
     res_hbm, mem_hbm, wx_hbm, wy_hbm,
-    out_ref,
-    res, mt, a0, a1, w1, w2, c0, ax, ay, own, strip, sides, mr, ml, ql, qr, gt, g,
-    row_out, row_in, proj, proj_out, proj_in, sx, pk_r, pk_l, cl, cr, band, z,
-    wx_ref, wy_ref, own_sem, res_sem, wind_sem, m_send, m_recv, h_send, h_recv, r_send, r_recv, p_send, p_recv, c_send, c_recv,
+    out_hbm,
+    res, mt, a0, a1, w1, w2, w3, c0, ax, ay, own, strip, sides, powers, mr, ml, ql, qr, gt, g,
+    row_out, row_in, proj, proj_out, proj_in, sx, pk_r, pk_l, cl, cr, band, z, half_ref,
+    wx_ref, wy_ref, own_sem, res_sem, wind_sem, out_sem, m_send, m_recv, h_send, h_recv, r_send, r_recv, p_send, p_recv, c_send, c_recv,
 ):
     t = lax.axis_index("tile")
     m = lax.axis_index("member")
@@ -120,6 +121,7 @@
     def _():
         for a in (a0, a1):
             a[pl.ds(0, HALO * LEV), :] = jnp.zeros((HALO * LEV, COLS), F32)
+        own[:, 0:HALO] = jnp.zeros((2, HALO, 8, COLS), F32)
         ql[:, 0] = jnp.zeros((2, 8, COLS), F32)
         qr[:, 0] = jnp.zeros((2, 8, COLS), F32)
         proj[:, :, 0:REACH, :] = jnp.zeros((2, 16, REACH, COLS), F32)
@@ -130,6 +132,7 @@
     def _():
         for a in (a0, a1):
             a[pl.ds((HALO + ROWS) * LEV, HALO * LEV), :] = jnp.zeros((HALO * LEV, COLS), F32)
+        own[:, HALO + ROWS :] = jnp.zeros((2, HALO, 8, COLS), F32)
         ql[:, 5] = jnp.zeros((2, 8, COLS), F32)
         qr[:, 5] = jnp.zeros((2, 8, COLS), F32)
         proj[:, :, REACH + ROWS :, :] = jnp.zeros((2, 16, REACH, COLS), F32)
@@ -185,7 +188,10 @@
     def quad_copy(it, d):
         dt, dm = SIDES[d]
         src, dst = (mr.at[it], ql.at[it]) if dm > 0 else (ml.at[it], qr.at[it])
-        if dt == 0:
+        if dm == 0:
+            src = own.at[it, pl.ds(ROWS if dt > 0 else HALO, HALO)]
+            dst = own.at[it, pl.ds(0 if dt > 0 else HALO + ROWS, HALO)]
+        elif dt == 0:
             src, dst = src, dst.at[pl.ds(1, 4)]
         elif dt > 0:
             src, dst = src.at[pl.ds(3, 1)], dst.at[pl.ds(0, 1)]
@@ -216,21 +222,31 @@
         a = (a0, a1)[it]
 
         def pack(r, carry):
-            own[HALO + r] = edges(a, HALO + r)
+            own[it, HALO + r] = edges(a, HALO + r)
             return carry
 
-        lax.fori_loop(0, ROWS, pack, 0, unroll=8 if it else 2)
-        for quad in range(4):
-            right = jnp.zeros((8, COLS), F32)
-            left = jnp.zeros((8, COLS), F32)
-            for k in range(4):
-                v = own[HALO + 4 * quad + k]
-                here = q // 4 == k
-                right = jnp.where(here, pltpu.roll(v, (4 * k - 8) % COLS, 1), right)
-                left = jnp.where(here, pltpu.roll(v, (4 * k - 4) % COLS, 1), left)
-            mr[it, quad] = right
-            ml[it, quad] = left
-        for d in range(2, 8):
+        def pack_ends(r, carry):
+            return pack(r + ROWS - HALO, pack(r, carry))
+
+        def quads(numbers):
+            for quad in numbers:
+                right = jnp.zeros((8, COLS), F32)
+                left = jnp.zeros((8, COLS), F32)
+                for k in range(4):
+                    v = own[it, HALO + 4 * quad + k]
+                    here = q // 4 == k
+                    right = jnp.where(here, pltpu.roll(v, (4 * k - 8) % COLS, 1), right)
+                    left = jnp.where(here, pltpu.roll(v, (4 * k - 4) % COLS, 1), left)
+                mr[it, quad] = right
+                ml[it, quad] = left
+
+        lax.fori_loop(0, HALO, pack_ends, 0, unroll=HALO if it else 1)
+        quads((0, 3))
+        for d in (4, 5, 6, 7, 0, 1):
+            guarded(there(*SIDES[d]), quad_copy(it, d).start)
+        lax.fori_loop(HALO, ROWS - HALO, pack, 0, unroll=ROWS - 2 * HALO if it else 1)
+        quads((1, 2))
+        for d in (2, 3):
             guarded(there(*SIDES[d]), quad_copy(it, d).start)
 
     res_copy.wait()
@@ -291,87 +307,110 @@
     )
     strip_mask = jnp.where(inside, 1.0, 0.0).astype(F32)
 
-    def adjoint(it):
+    binomial = (1.0, 4.0, 6.0, 4.0, 1.0)
+
+    def column_powers(a, r, most):
+        for k in range(GROUPS):
+            here = pl.ds(pl.multiple_of(r * LEV + 8 * k, 8), 8)
+            x = a[here, :]
+            for power in range(1, most + 1):
+                left = jnp.where(lane == 0, 0.0, pltpu.roll(x, 1, 1))
+                right = jnp.where(lane == COLS - 1, 0.0, pltpu.roll(x, COLS - 1, 1))
+                x = left + ay[8 * k : 8 * k + 8, :] * right
+                powers[power - 1, here, :] = x
+
+    def adjoint_early(it):
+        def row(r, carry):
+            column_powers((a0, a1)[it], r, STEPS)
+            return carry
+
+        lax.fori_loop(HALO, HALO + ROWS, row, 0, unroll=4 if it else 1)
+        for stage in range(1, STEPS + 1):
+            lax.fori_loop(
+                HALO + stage, HALO + ROWS - stage, functools.partial(row_stage, it, stage), 0,
+                unroll=2 if it else 1,
+            )
+
+    def row_stage(it, stage, r, carry, scale=None):
+        src = ((a0, a1)[it], w1, w2, w3)[stage - 1]
+        dst = (w1, w2, w3, gt)[stage - 1]
+        for k in range(GROUPS):
+            at = r * LEV + 8 * k
+            here = pl.ds(pl.multiple_of(at, 8), 8)
+            s = slice(8 * k, 8 * k + 8)
+            out = (
+                c0[s, :] * src[here, :]
+                + src[pl.ds(pl.multiple_of(at - LEV, 8), 8), :]
+                + ax[s, :] * src[pl.ds(pl.multiple_of(at + LEV, 8), 8), :]
+            )
+            side = powers[stage - 1, here, :]
+            out = out + (side if stage == STEPS else binomial[stage] * side)
+            if scale is not None:
+                out = out * scale
+            if stage == STEPS:
+                dst[pl.ds(pl.multiple_of(at - HALO * LEV, 8), 8), :] = out
+            else:
+                dst[here, :] = out
+        return carry
+
+    def adjoint_late(it):
         a = (a0, a1)[it]
         receive_rows(it)
-        for d in range(2, 8):
+        for r in range(1, HALO):
+            column_powers(a, r, r)
+            column_powers(a, XROWS - 1 - r, r)
+        for stage in range(1, STEPS + 1):
+            for r in range(stage, HALO + stage):
+                row_stage(it, stage, r, 0, row_low if r < HALO else None)
+                r = XROWS - 1 - r
+                row_stage(it, stage, r, 0, row_high if r >= HALO + ROWS else None)
+
+        for d in range(8):
             dt, dm = SIDES[d]
             guarded(there(-dt, -dm), quad_copy(it, d).wait_recv)
-
-        def pack(r, carry):
-            own[r] = edges(a, r)
-            own[r + HALO + ROWS] = edges(a, r + HALO + ROWS)
-            return carry
-
-        lax.fori_loop(0, HALO, pack, 0, unroll=HALO if it else 1)
         for r in range(XROWS):
             left = pltpu.roll(ql[it, r // 4], (-4 * (r % 4)) % COLS, 1)
             right = pltpu.roll(qr[it, r // 4], (12 - 4 * (r % 4)) % COLS, 1)
-            strip[0, r] = jnp.where(q < 4, left, jnp.where(q >= 12, right, own[r]))
+            strip[0, r] = jnp.where(q < 4, left, jnp.where(q >= 12, right, own[it, r]))
         sc0, sax, say = strip_coefficient(c0), strip_coefficient(ax), strip_coefficient(ay)
-        for step in range(1, STEPS):
+        mine = jnp.logical_and(q >= 4, q < 12)
+
+        def strip_step(load, r):
+            v = load(r)
+            out = (
+                sc0 * v
+                + (load(r - 1) + pltpu.roll(v, 1, 1))
+                + sax * load(r + 1)
+                + say * pltpu.roll(v, COLS - 1, 1)
+            )
+            return out * row_low if r < HALO else out * row_high if r >= HALO + ROWS else out
+
+        for step in range(1, STEPS + 1):
+
+            def joined(r):
+                outer = strip[step - 1, r]
+                return jnp.where(mine, 0.0 if step == 1 else sides[step - 2, r], outer)
+
             for r in range(step, XROWS - step):
-                v = strip[step - 1, r]
-                out = (
-                    sc0 * v
-                    + (strip[step - 1, r - 1] + pltpu.roll(v, 1, 1))
-                    + sax * strip[step - 1, r + 1]
-                    + say * pltpu.roll(v, COLS - 1, 1)
-                ) * strip_mask
-                if r < HALO:
-                    out = out * row_low
-                elif r >= HALO + ROWS:
-                    out = out * row_high
-                strip[step, r] = out
-        for step in range(STEPS):
-            for r in range(step + 1, XROWS - step - 1):
-                v = strip[step, r]
-                sides[step, r] = jnp.where(
-                    q == 0, pltpu.roll(v, COLS - 12, 1), pltpu.roll(v, COLS - 2, 1)
+                sides[step - 1, r] = strip_step(joined, r)
+                if step < STEPS:
+                    strip[step, r] = strip_step(lambda i: strip[step - 1, i], r) * strip_mask
+
+        def finish(r, carry):
+            v = sides[STEPS - 1, HALO + r]
+            v = jnp.where(q < 4, pltpu.roll(v, COLS - 8, 1), v)
+            for k in range(GROUPS):
+                here = pl.ds(pl.multiple_of(r * LEV + 8 * k, 8), 8)
+                ends = jnp.where(
+                    jnp.logical_or(lane < HALO, lane >= COLS - HALO),
+                    pltpu.roll(v, COLS - HALO - 16 * k, 1),
+                    0.0,
                 )
-        for step in range(1, STEPS + 1):
-            src = (a, w1, w2, w1)[step - 1]
-            dst = (w1, w2, w1, gt)[step - 1]
-
-            def row(r, carry, scale=None):
-                side = sides[step - 1, r]
-                for k in range(GROUPS):
-                    at = r * LEV + 8 * k
-                    here = pl.ds(pl.multiple_of(at, 8), 8)
-                    v = src[here, :]
-                    up = src[pl.ds(pl.multiple_of(at - LEV, 8), 8), :]
-                    down = src[pl.ds(pl.multiple_of(at + LEV, 8), 8), :]
-                    ends = pltpu.roll(side, COLS - 1 - 16 * k, 1)
-                    left = jnp.where(lane == 0, ends, pltpu.roll(v, 1, 1))
-                    right = jnp.where(lane == COLS - 1, ends, pltpu.roll(v, COLS - 1, 1))
-                    s = slice(8 * k, 8 * k + 8)
-                    out = c0[s, :] * v + (up + left) + ax[s, :] * down + ay[s, :] * right
-                    if scale is not None:
-                        out = out * scale
-                    if step == STEPS:
-                        out = (out * diffusion**STEPS).astype(BF16).astype(F32)
-                        dst[pl.ds(pl.multiple_of(at - HALO * LEV, 8), 8), :] = out
-                    else:
-                        dst[here, :] = out
-                return carry
-
-            if step < STEPS:
-                lax.fori_loop(
-                    step, HALO, functools.partial(row, scale=row_low), 0, unroll=True if it else 1
-                )
-            lax.fori_loop(HALO, HALO + ROWS, row, 0, unroll=ROWS if it else 2)
-            if step < STEPS:
-                lax.fori_loop(
-                    HALO + ROWS, XROWS - step, functools.partial(row, scale=row_high), 0,
-                    unroll=True if it else 1,
-                )
-
-        def gather(l, carry):
-            g[l, 0:8, :] = gt[pl.ds(l, 8, stride=LEV), :]
-            g[l, 8:16, :] = gt[pl.ds(8 * LEV + l, 8, stride=LEV), :]
+                out = (gt[here, :] + ends) * diffusion**STEPS
+                g[pl.ds(8 * k * ROWS + r, 8, stride=ROWS), :] = out.astype(BF16).astype(F32)
             return carry
 
-        lax.fori_loop(0, LEV, gather, 0, unroll=4)
+        lax.fori_loop(0, ROWS, finish, 0, unroll=4 if it else 1)
 
     own_rows = pl.ds(REACH, ROWS)
 
@@ -382,7 +421,7 @@
             start = (proj[it, 2 * pair, own_rows, :], proj[it, 2 * pair + 1, own_rows, :])
 
         def level(l, sums):
-            v = g[l]
+            v = g[pl.ds(pl.multiple_of(l * ROWS, ROWS), ROWS), :]
             return tuple(s + mt[pair, n, l].astype(F32) * v for n, s in enumerate(sums))
 
         sums = lax.fori_loop(first, first + count, level, start, unroll=8)
@@ -491,6 +530,10 @@
                         ),
                     )
 
+    def out_copy(part):
+        levels = pl.ds(part * (LEV // PARTS), LEV // PARTS)
+        return pltpu.make_async_copy(half_ref.at[levels], out_hbm.at[levels], out_sem.at[part])
+
     def increments(it):
         width = 4
 
@@ -505,21 +548,41 @@
                 l = width * step + i
                 if it == 0:
                     half = relax * sums[i]
-                    out_ref[l] = half
+                    half_ref[l] = half
                     v = res[l] - half
                     a1[pl.ds(HALO * LEV + l, 8, stride=LEV), :] = v[0:8]
                     a1[pl.ds((HALO + 8) * LEV + l, 8, stride=LEV), :] = v[8:16]
                 else:
-                    out_ref[l] = out_ref[l] + relax * sums[i]
+                    half_ref[l] = half_ref[l] + relax * sums[i]
             return carry
 
-        for half in range(HALVES):
-            first = half * HLEV // width
-            lax.fori_loop(first, first + HLEV // width, levels, 0)
+        parts = PARTS if it else HALVES
+        for part in range(parts):
+            count = LEV // parts // width
+            lax.fori_loop(part * count, (part + 1) * count, levels, 0)
             if it == 0:
-                send_rows(1, half)
-
-    adjoint(0)
+                send_rows(1, part)
+            else:
+                out_copy(part).start()
+
+    def halos_sent(it):
+        for d in (0, 1):
+            for half in range(HALVES):
+                guarded(there(*SIDES[d]), row_copy(it, d, half).wait_send)
+        for d in range(8):
+            guarded(there(*SIDES[d]), quad_copy(it, d).wait_send)
+
+    def projects_sent(it):
+        for slot in range(8):
+            for d in (0, 1):
+                guarded(there(*SIDES[d]), project_copy(it, pairs[slot], slot, d).wait_send)
+
+    def columns_sent(it):
+        for d, side in enumerate(COLUMN_SIDES):
+            guarded(there(*side), column_copy(it, d).wait_send)
+
+    adjoint_early(0)
+    adjoint_late(0)
     own_copy.wait()
     project(0, pairs[0], 0, LEV, True)
     send_project(0, 0)
@@ -535,29 +598,26 @@
     increments(0)
 
     send_halos(1)
-    adjoint(1)
+    adjoint_early(1)
+    for i, c in ORDER:
+        member_copy(i, c).wait_send()
+    halos_sent(0)
+    projects_sent(0)
+    columns_sent(0)
+    adjoint_late(1)
     for slot in range(8):
         project(1, pairs[slot], 0, LEV, True)
         send_project(1, slot)
     send_columns(1)
+    halos_sent(1)
     for slot in range(8):
         smooth_rows(1, slot)
+    projects_sent(1)
     smooth_columns(1)
     increments(1)
-
-    for i, c in ORDER:
-        member_copy(i, c).wait_send()
-    for it in range(2):
-        for d in (0, 1):
-            for half in range(HALVES):
-                guarded(there(*SIDES[d]), row_copy(it, d, half).wait_send)
-        for d in range(2, 8):
-            guarded(there(*SIDES[d]), quad_copy(it, d).wait_send)
-        for slot in range(8):
-            for d in (0, 1):
-                guarded(there(*SIDES[d]), project_copy(it, pairs[slot], slot, d).wait_send)
-        for d, side in enumerate(COLUMN_SIDES):
-            guarded(there(*side), column_copy(it, d).wait_send)
+    columns_sent(1)
+    for part in range(PARTS):
+        out_copy(part).wait()
 
 
 def per_device(tiles, blocks, residual_in, members, wind_x, wind_y):
@@ -570,19 +630,20 @@
         functools.partial(kernel, tiles, blocks),
         out_shape=jax.ShapeDtypeStruct((LEV, ROWS, COLS), F32),
         in_specs=[anywhere] * 4,
-        out_specs=pl.BlockSpec(memory_space=vmem),
+        out_specs=anywhere,
         scratch_shapes=[
             vmem((LEV, ROWS, COLS), F32),
             vmem((8, 2, LEV, ROWS, COLS), BF16),
-            extended, extended, extended, extended,
+            extended, extended, extended, extended, extended,
             coefficient, coefficient, coefficient,
-            vmem((XROWS, 8, COLS), F32),
+            vmem((2, XROWS, 8, COLS), F32),
             vmem((STEPS, XROWS, 8, COLS), F32),
             vmem((STEPS, XROWS, 8, COLS), F32),
+            vmem((STEPS, XROWS * LEV, COLS), F32),
             vmem((2, 4, 8, COLS), F32), vmem((2, 4, 8, COLS), F32),
             vmem((2, 6, 8, COLS), F32), vmem((2, 6, 8, COLS), F32),
             vmem((ROWS * LEV, COLS), F32),
-            vmem((LEV, ROWS, COLS), F32),
+            vmem((LEV * ROWS, COLS), F32),
             vmem((2, 2, HALVES, HALO * HLEV, COLS), BF16),
             vmem((2, 2, HALVES, HALO * HLEV, COLS), BF16),
             vmem((2, 16, ROWS + 2 * REACH, COLS), F32),
@@ -594,8 +655,9 @@
             vmem((2, 2, ROWS + 2 * REACH, COLS), F32),
             vmem((3, 2, COLS, COLS), BF16),
             vmem((16 * ROWS, COLS), F32),
+            vmem((LEV, ROWS, COLS), F32),
             pltpu.SMEM((LEV,), F32), pltpu.SMEM((LEV,), F32),
-            pltpu.SemaphoreType.DMA, pltpu.SemaphoreType.DMA, dma(2),
+            pltpu.SemaphoreType.DMA, pltpu.SemaphoreType.DMA, dma(2), dma(PARTS),
             dma(len(FLOWS), CHUNKS), dma(len(FLOWS), CHUNKS),
             dma(2, 8), dma(2, 8),
             dma(2, 2, HALVES), dma(2, 2, HALVES),

time: 84.3 us -> 82.7 us (0.981)
  Pallas kernels: 81.4 us -> 79.7 us
    pallas_call x1, Pallas kernels: 81.4 us -> 79.7 us  [per_device(): pl.pallas_call(functools.partial(kernel, tiles, blocks), out_shape=jax.Sh...]
where the time goes in v5:
time: 82.7 us; the launch traced here: 82.5 us
  Pallas kernels  79.7 us (96%)
  other arithmetic  2.08 us (3%)
    pallas_call x1, Pallas kernels, per_device(): pl.pallas_call(functools.partial(kernel, tiles, blocks), out_shape=jax.Sh...  79.7 us
    sub x1, other arithmetic, per_device(): return (half * (1.0 / relax), residual_in - half)  2.08 us

profile of v5, /device:TPU:29, one launch (start us, length us, event | category | flops | bytes accessed | tf_op | source)
XLA Modules:
  0.0 82.5 jit_solution(17310878112210906944)
XLA Ops:
  0.6 0.0 copy-start
  0.6 79.7 %ensemble_step.1 = f32[64,16,128]{2,1,0:T(8,128)} custom-call(f32[64,16,128]{2,1,0:T(8,128)} %res_hbm.1, bf16[2,64,16,1024]{3,2,1,0:T(8,128)(2,1)} %mem_hbm.1, f32[64]{0:T(128)} %wx_hbm.1, f32[64]{0:T(128)} %wy_hbm.1), custom_call_target="tpu_custom_call" | custom-call | tf_op jit(solution)/shard_map/ensemble_step/pallas_call | solution.py:629
  80.4 0.0 copy-done
  80.4 2.1 %fusion = (f32[64,16,128]{2,1,0:T(8,128)}, f32[64,16,128]{2,1,0:T(8,128)}) fusion(f32[64,16,128]{2,1,0:T(8,128)S(1)} %copy-done, f32[64,16,128]{2,1,0:T(8,128)} %ensemble_step.1), kind=kLoop, calls=%fused_computation.1 | loop fusion | flops 262144 | bytes 2097152 | tf_op jit(solution)/shard_map/sub | solution.py:670
Async XLA Ops:
  0.6 79.8 %copy-start = (f32[64,16,128]{2,1,0:T(8,128)S(1)}, f32[64,16,128]{2,1,0:T(8,128)}, u32[]{:S(2)}) copy-start(f32[64,16,128]{2,1,0:T(8,128)} %res_hbm.1) | copy-start | bytes 1572868

commit v6 on v5

--- a/solution.py
+++ b/solution.py
@@ -49,7 +49,7 @@
     res_hbm, mem_hbm, wx_hbm, wy_hbm,
     out_hbm,
     res, mt, a0, a1, w1, w2, w3, c0, ax, ay, own, strip, sides, powers, mr, ml, ql, qr, gt, g,
-    row_out, row_in, proj, proj_out, proj_in, sx, pk_r, pk_l, cl, cr, band, z, half_ref,
+    row_out, row_in, proj, proj_out, proj_in, sx, pk_r, pk_l, cl_in, cr_in, cl, cr, band, z, half_ref,
     wx_ref, wy_ref, own_sem, res_sem, wind_sem, out_sem, m_send, m_recv, h_send, h_recv, r_send, r_recv, p_send, p_recv, c_send, c_recv,
 ):
     t = lax.axis_index("tile")
@@ -324,7 +324,7 @@
             column_powers((a0, a1)[it], r, STEPS)
             return carry
 
-        lax.fori_loop(HALO, HALO + ROWS, row, 0, unroll=4 if it else 1)
+        lax.fori_loop(HALO, HALO + ROWS, row, 0, unroll=2 if it else 1)
         for stage in range(1, STEPS + 1):
             lax.fori_loop(
                 HALO + stage, HALO + ROWS - stage, functools.partial(row_stage, it, stage), 0,
@@ -436,14 +436,14 @@
             device_id=peer(*SIDES[d]), device_id_type=MESH,
         )
 
-    pairs = [m] + [mate(-dy, dz) for dy, dz in FLOWS]
+    order = ([m] + [mate(-dy, dz) for dy, dz in FLOWS], list(range(8)))
 
     def send_project(it, slot):
         for n in range(2):
-            member = 2 * pairs[slot] + n
+            member = 2 * order[it][slot] + n
             proj_out[it, member] = proj[it, member, own_rows, :].astype(BF16)
         for d in (0, 1):
-            guarded(there(*SIDES[d]), project_copy(it, pairs[slot], slot, d).start)
+            guarded(there(*SIDES[d]), project_copy(it, order[it][slot], slot, d).start)
 
     def taper(ref, lead, at):
         total = w[REACH] * ref[(*lead, pl.ds(at, 8), slice(None))]
@@ -455,7 +455,7 @@
         return total
 
     def smooth_rows(it, slot):
-        pair = pairs[slot]
+        pair = order[it][slot]
         for d in (0, 1):
 
             def unpack(d=d):
@@ -473,29 +473,48 @@
                     proj, (it, 2 * pair + n), REACH + half
                 )
 
-    def column_copy(it, d):
+    def column_copy(it, d, part):
         dt, dm = COLUMN_SIDES[d]
-        src, dst = (pk_r.at[it], cl.at[it]) if dm > 0 else (pk_l.at[it], cr.at[it])
+        src, dst = (pk_r, cl_in) if dm > 0 else (pk_l, cr_in)
         return pltpu.make_async_remote_copy(
-            src_ref=src,
-            dst_ref=dst.at[:, pl.ds(REACH if dt == 0 else 0 if dt > 0 else REACH + ROWS, ROWS)],
-            send_sem=c_send.at[it, d], recv_sem=c_recv.at[it, d],
+            src_ref=src.at[it, part],
+            dst_ref=dst.at[it, part, column_place(dt)],
+            send_sem=c_send.at[it, d, part], recv_sem=c_recv.at[it, d, part],
             device_id=peer(dt, dm), device_id_type=MESH,
         )
 
-    def send_columns(it):
-        for part in range(2):
-            for half in (0, 8):
-                right = jnp.zeros((8, COLS), F32)
-                left = jnp.zeros((8, COLS), F32)
-                for n in range(8):
-                    v = proj[it, 8 * part + n, REACH + half : REACH + half + 8, :]
-                    right = jnp.where(group == n, pltpu.roll(v, (16 * n - 112) % COLS, 1), right)
-                    left = jnp.where(group == n, pltpu.roll(v, 16 * n, 1), left)
-                pk_r[it, part, half : half + 8, :] = right
-                pk_l[it, part, half : half + 8, :] = left
+    def column_place(dt):
+        return 1 if dt == 0 else 0 if dt > 0 else 2
+
+    def send_columns(it, part):
+        rights, lefts = [], []
+        for half in (0, 8):
+            right = jnp.zeros((8, COLS), F32)
+            left = jnp.zeros((8, COLS), F32)
+            for n in range(8):
+                v = proj[it, 8 * part + n, REACH + half : REACH + half + 8, :]
+                right = jnp.where(group == n, pltpu.roll(v, (16 * n - 112) % COLS, 1), right)
+                left = jnp.where(group == n, pltpu.roll(v, 16 * n, 1), left)
+            rights.append(right)
+            lefts.append(left)
+        pk_r[it, part] = jnp.concatenate(rights).astype(BF16)
+        pk_l[it, part] = jnp.concatenate(lefts).astype(BF16)
         for d, side in enumerate(COLUMN_SIDES):
-            guarded(there(*side), column_copy(it, d).start)
+            guarded(there(*side), column_copy(it, d, part).start)
+
+    def receive_columns(it):
+        for d, (dt, dm) in enumerate(COLUMN_SIDES):
+
+            def unpack(d=d, dt=dt, dm=dm):
+                place = column_place(dt)
+                got, to = (cl_in, cl) if dm > 0 else (cr_in, cr)
+                for part in range(2):
+                    column_copy(it, d, part).wait_recv()
+                    to[it, part, place * REACH : (place + 1) * REACH, :] = got[
+                        it, part, place
+                    ].astype(F32)
+
+            guarded(there(-dt, -dm), unpack)
 
     def split(x):
         high = x.astype(BF16)
@@ -508,8 +527,7 @@
 
     def smooth_columns(it):
         z[...] = times(sx[...], 0)
-        for d, (dt, dm) in enumerate(COLUMN_SIDES):
-            guarded(there(-dt, -dm), column_copy(it, d).wait_recv)
+        receive_columns(it)
         outer = []
         for which, ref in ((1, cl), (2, cr)):
             x = jnp.concatenate(
@@ -575,23 +593,25 @@
     def projects_sent(it):
         for slot in range(8):
             for d in (0, 1):
-                guarded(there(*SIDES[d]), project_copy(it, pairs[slot], slot, d).wait_send)
+                guarded(there(*SIDES[d]), project_copy(it, order[it][slot], slot, d).wait_send)
 
     def columns_sent(it):
         for d, side in enumerate(COLUMN_SIDES):
-            guarded(there(*side), column_copy(it, d).wait_send)
+            for part in range(2):
+                guarded(there(*side), column_copy(it, d, part).wait_send)
 
     adjoint_early(0)
     adjoint_late(0)
     own_copy.wait()
-    project(0, pairs[0], 0, LEV, True)
+    project(0, order[0][0], 0, LEV, True)
     send_project(0, 0)
     for i, c in ORDER:
         member_copy(i, c).wait_recv()
-        project(0, pairs[1 + i], c * CLEV, CLEV, c == 0)
+        project(0, order[0][1 + i], c * CLEV, CLEV, c == 0)
         if c == CHUNKS - 1:
             send_project(0, 1 + i)
-    send_columns(0)
+    for part in range(2):
+        send_columns(0, part)
     for slot in range(8):
         smooth_rows(0, slot)
     smooth_columns(0)
@@ -606,9 +626,10 @@
     columns_sent(0)
     adjoint_late(1)
     for slot in range(8):
-        project(1, pairs[slot], 0, LEV, True)
+        project(1, slot, 0, LEV, True)
         send_project(1, slot)
-    send_columns(1)
+        if slot % 4 == 3:
+            send_columns(1, slot // 4)
     halos_sent(1)
     for slot in range(8):
         smooth_rows(1, slot)
@@ -650,7 +671,9 @@
             vmem((2, 16, ROWS, COLS), BF16),
             vmem((2, 2, 16, REACH, COLS), BF16),
             vmem((16 * ROWS, COLS), F32),
-            vmem((2, 2, ROWS, COLS), F32), vmem((2, 2, ROWS, COLS), F32),
+            vmem((2, 2, ROWS, COLS), BF16), vmem((2, 2, ROWS, COLS), BF16),
+            vmem((2, 2, 3, REACH, COLS), BF16),
+            vmem((2, 2, 3, REACH, COLS), BF16),
             vmem((2, 2, ROWS + 2 * REACH, COLS), F32),
             vmem((2, 2, ROWS + 2 * REACH, COLS), F32),
             vmem((3, 2, COLS, COLS), BF16),
@@ -662,7 +685,7 @@
             dma(2, 8), dma(2, 8),
             dma(2, 2, HALVES), dma(2, 2, HALVES),
             dma(2, 8, 2), dma(2, 8, 2),
-            dma(2, len(COLUMN_SIDES)), dma(2, len(COLUMN_SIDES)),
+            dma(2, len(COLUMN_SIDES), 2), dma(2, len(COLUMN_SIDES), 2),
         ],
         compiler_params=pltpu.CompilerParams(collective_id=0, has_side_effects=True),
         name="ensemble_step",

time: 82.7 us -> 82.1 us (level)
  no operation moved by 1% of the time
where the time goes in v6:
time: 82.1 us; the launch traced here: 81.9 us
  Pallas kernels  79.2 us (96%)
  other arithmetic  2.08 us (3%)
    pallas_call x1, Pallas kernels, per_device(): pl.pallas_call(functools.partial(kernel, tiles, blocks), out_shape=jax.Sh...  79.2 us
    sub x1, other arithmetic, per_device(): return (half * (1.0 / relax), residual_in - half)  2.08 us

profile of v6, /device:TPU:29, one launch (start us, length us, event | category | flops | bytes accessed | tf_op | source)
XLA Modules:
  0.0 81.9 jit_solution(8052693607330258843)
XLA Ops:
  0.6 0.0 copy-start
  0.6 79.2 %ensemble_step.1 = f32[64,16,128]{2,1,0:T(8,128)} custom-call(f32[64,16,128]{2,1,0:T(8,128)} %res_hbm.1, bf16[2,64,16,1024]{3,2,1,0:T(8,128)(2,1)} %mem_hbm.1, f32[64]{0:T(128)} %wx_hbm.1, f32[64]{0:T(128)} %wy_hbm.1), custom_call_target="tpu_custom_call" | custom-call | tf_op jit(solution)/shard_map/ensemble_step/pallas_call | solution.py:650
  79.8 0.0 copy-done
  79.8 2.1 %fusion = (f32[64,16,128]{2,1,0:T(8,128)}, f32[64,16,128]{2,1,0:T(8,128)}) fusion(f32[64,16,128]{2,1,0:T(8,128)S(1)} %copy-done, f32[64,16,128]{2,1,0:T(8,128)} %ensemble_step.1), kind=kLoop, calls=%fused_computation.1 | loop fusion | flops 262144 | bytes 2097152 | tf_op jit(solution)/shard_map/sub | solution.py:693
Async XLA Ops:
  0.6 79.2 %copy-start = (f32[64,16,128]{2,1,0:T(8,128)S(1)}, f32[64,16,128]{2,1,0:T(8,128)}, u32[]{:S(2)}) copy-start(f32[64,16,128]{2,1,0:T(8,128)} %res_hbm.1) | copy-start | bytes 1572868

commit v7 on v6

--- a/solution.py
+++ b/solution.py
@@ -426,6 +426,19 @@
 
         sums = lax.fori_loop(first, first + count, level, start, unroll=8)
         for n in range(2):
+            proj[it, 2 * pair + n, own_rows, :] = sums[n]
+
+    def project_both(it, pair):
+        def level(l, sums):
+            v = g[pl.ds(pl.multiple_of(l * ROWS, ROWS), ROWS), :]
+            return tuple(
+                s + mt[pair + n // 2, n % 2, l].astype(F32) * v for n, s in enumerate(sums)
+            )
+
+        sums = lax.fori_loop(
+            0, LEV, level, tuple(jnp.zeros((ROWS, COLS), F32) for _ in range(4)), unroll=8
+        )
+        for n in range(4):
             proj[it, 2 * pair + n, own_rows, :] = sums[n]
 
     def project_copy(it, pair, slot, d):
@@ -626,7 +639,8 @@
     columns_sent(0)
     adjoint_late(1)
     for slot in range(8):
-        project(1, slot, 0, LEV, True)
+        if slot % 2 == 0:
+            project_both(1, slot)
         send_project(1, slot)
         if slot % 4 == 3:
             send_columns(1, slot // 4)

time: 82.1 us -> 81.9 us (level)
  no operation moved by 1% of the time
where the time goes in v7:
time: 81.9 us; the launch traced here: 81.8 us
  Pallas kernels  79 us (96%)
  other arithmetic  2.08 us (3%)
    pallas_call x1, Pallas kernels, per_device(): pl.pallas_call(functools.partial(kernel, tiles, blocks), out_shape=jax.Sh...  79 us
    sub x1, other arithmetic, per_device(): return (half * (1.0 / relax), residual_in - half)  2.08 us

profile of v7, /device:TPU:29, one launch (start us, length us, event | category | flops | bytes accessed | tf_op | source)
XLA Modules:
  0.0 81.8 jit_solution(13446883706845277844)
XLA Ops:
  0.6 0.0 copy-start
  0.6 79.0 %ensemble_step.1 = f32[64,16,128]{2,1,0:T(8,128)} custom-call(f32[64,16,128]{2,1,0:T(8,128)} %res_hbm.1, bf16[2,64,16,1024]{3,2,1,0:T(8,128)(2,1)} %mem_hbm.1, f32[64]{0:T(128)} %wx_hbm.1, f32[64]{0:T(128)} %wy_hbm.1), custom_call_target="tpu_custom_call" | custom-call | tf_op jit(solution)/shard_map/ensemble_step/pallas_call | solution.py:664
  79.7 0.0 copy-done
  79.7 2.1 %fusion = (f32[64,16,128]{2,1,0:T(8,128)}, f32[64,16,128]{2,1,0:T(8,128)}) fusion(f32[64,16,128]{2,1,0:T(8,128)S(1)} %copy-done, f32[64,16,128]{2,1,0:T(8,128)} %ensemble_step.1), kind=kLoop, calls=%fused_computation.1 | loop fusion | flops 262144 | bytes 2097152 | tf_op jit(solution)/shard_map/sub | solution.py:707
Async XLA Ops:
  0.6 79.1 %copy-start = (f32[64,16,128]{2,1,0:T(8,128)S(1)}, f32[64,16,128]{2,1,0:T(8,128)}, u32[]{:S(2)}) copy-start(f32[64,16,128]{2,1,0:T(8,128)} %res_hbm.1) | copy-start | bytes 1572868
